TPU v7x, 1024 devices: a whole 4x8x16 slice. The times are simulated.
1024 devices in a mesh: dp: 32 (over z, x_hi), expert: 32 (over x_lo, y, core).
Axes of the slice: x: 4 (x_hi: 2, x_lo: 2; x = x_hi * 2 + x_lo), y: 8, z: 16, core: 2. Of those that a mesh axis runs over, the one named last changes fastest.
Arguments:
- grad_output: bfloat16 [4096, 6144], P('expert', 'dp'), may hold values from -6 to 6
- gate_probs: float32 [4096, 4], P('expert'), may hold values from 0.05 to 1
- routing: int32 [4096, 4], P('expert'), may hold values from 0 to 127, all different within a row; in each aligned block of 128 rows (0 to 127, 128 to 255, ...) at most 5 rows name the same one
- old_weights: bfloat16 [128, 1024, 6144], P('expert', None, 'dp'), may hold values from -0.1875 to 0.1875
- old_slot_expert: int32 [128], replicated, may hold values from 0 to 127, each once
- new_slot_expert: int32 [128], replicated, may hold values from 0 to 127, each once
- saved_hidden: bfloat16 [128, 160, 1024], P('expert'), may hold values from -6 to 6
- shared_hidden: bfloat16 [4096, 1024], P('expert'), may hold values from -6 to 6
- shared_weight: bfloat16 [1024, 6144], P('expert', 'dp'), may hold values from -0.1875 to 0.1875
Outputs:
- expert_weight_grad: bfloat16 [128, 1024, 6144], P('expert', None, 'dp')
- expert_hidden_grad: bfloat16 [128, 160, 1024], P('expert', 'dp')
- shared_hidden_grad: bfloat16 [4096, 1024], P('expert', 'dp')
- shared_weight_grad: bfloat16 [1024, 6144], P('expert', 'dp')
Inputs may be any that keep to these rules, and one draw needn't show every extreme that they name: `routing`: each row names 4 different experts. Among the 128 rows of one group no expert is named by more than 5 rows, a bound that some block reaches of them. `old_slot_expert`: A permutation of the experts. `new_slot_expert`: A permutation of the experts.
All inputs are finite; a program needn't handle non-finite values.
Results may differ from a plain program's by a relative error of at most 0.023.
Values may be sent and summed in bfloat16 or wider, within the bound.
No kernel may reach another device: no remote copies, remote signals or barrier semaphores. Data moves between devices by JAX's collectives and lax.ppermute only.
A program may use at most 32 MiB of HBM per device.

v0:
```python
import jax
import jax.numpy as jnp
from jax import lax
from jax.sharding import Mesh
from jax.sharding import PartitionSpec as P

DP = ("dp_0", "dp_1")


def joined_along(tiles, dim):
    tiles = jnp.moveaxis(tiles, 0, dim)
    dims = tiles.shape
    return tiles.reshape(*dims[:dim], dims[dim] * dims[dim + 1], *dims[dim + 2 :])


def from_everyone(array, axis):
    length = lax.axis_size(axis)
    return lax.all_to_all(
        jnp.broadcast_to(array[None], (length, *array.shape)), axis, 0, 0, tiled=True
    )


def collect(array, axis, dim):
    return joined_along(from_everyone(array, axis), dim)


def cut_along(array, dim, length):
    dims = array.shape
    tiles = array.reshape(*dims[:dim], length, dims[dim] // length, *dims[dim + 1 :])
    return jnp.moveaxis(tiles, dim, 0)


def sum_at_owner(array, axis, dim):
    length = lax.axis_size(axis)
    tiles = lax.all_to_all(cut_along(array, dim, length), axis, 0, 0, tiled=True)
    return jnp.sum(tiles.astype(jnp.float32), axis=0)


def sum_by_axis(array, axes, dim):
    for axis in axes:
        array = lax.psum_scatter(array, axis, scatter_dimension=dim, tiled=True)
    return array


def inverse_order(listing):
    labels = jnp.arange(listing.shape[0], dtype=jnp.int32)
    return jnp.sum(jnp.where(listing[None, :] == labels[:, None], labels[None, :], 0), axis=1)


def on_device(
    grad_output,
    gate_probs,
    routing,
    old_weights,
    old_slot_expert,
    new_slot_expert,
    saved_hidden,
    shared_hidden,
    shared_weight,
):
    groups = lax.axis_size("expert")
    local_experts, hidden, columns = old_weights.shape
    experts = old_slot_expert.shape[0]
    fragment = hidden // groups
    capacity = saved_hidden.shape[1] // groups
    tok_rows, chosen = routing.shape
    old_position = inverse_order(old_slot_expert)
    new_position = inverse_order(new_slot_expert)
    source_slot = jnp.take(old_position, new_slot_expert)
    pieces = old_weights.reshape(local_experts, groups, fragment, columns)
    spread = lax.all_to_all(pieces, "expert", split_axis=1, concat_axis=0, tiled=True)
    ordered = jnp.take(spread.reshape(experts, fragment, columns), source_slot, axis=0)
    ordered = ordered.reshape(groups, local_experts, fragment, columns)
    flat_routes = routing.reshape(-1)
    labels = jnp.arange(experts, dtype=jnp.int32)
    onehot = (flat_routes[:, None] == labels[None, :]).astype(jnp.int32)
    earlier = jnp.cumsum(onehot, axis=0) - onehot
    ranking = jnp.sum(earlier * onehot, axis=1)
    target = jnp.take(new_position, flat_routes) * capacity + ranking
    scaled = (grad_output.astype(jnp.float32)[:, None, :] * gate_probs[:, :, None]).astype(
        jnp.bfloat16
    )
    scaled = scaled.reshape(tok_rows * chosen, columns)
    outgoing = jnp.zeros((experts * capacity, columns), jnp.bfloat16).at[target].set(scaled)
    outgoing = outgoing.reshape(groups, local_experts, capacity, columns)
    relayed, received = (
        lax.all_to_all(ordered, "expert", split_axis=0, concat_axis=2, tiled=True),
        lax.all_to_all(outgoing, "expert", split_axis=0, concat_axis=2, tiled=True),
    )
    relayed = relayed.reshape(local_experts, hidden, columns)
    received = received.reshape(local_experts, groups * capacity, columns)
    weight_grad = jnp.einsum(
        "erf,erc->efc", saved_hidden, received, preferred_element_type=jnp.float32
    ).astype(jnp.bfloat16)
    routed_partial = jnp.einsum(
        "erc,efc->erf", received, relayed, preferred_element_type=jnp.float32
    )
    shared_partial = jnp.dot(
        grad_output, collect(shared_weight, "expert", 0).T, preferred_element_type=jnp.float32
    )
    shared_sum = sum_at_owner(
        jnp.dot(shared_hidden.T, grad_output, preferred_element_type=jnp.float32).astype(
            jnp.bfloat16
        ),
        "expert",
        0,
    )
    routed_sum, shared_hidden_sum = (
        sum_by_axis(routed_partial.astype(jnp.bfloat16), DP, 1).astype(jnp.float32),
        sum_by_axis(shared_partial.astype(jnp.bfloat16), DP, 1).astype(jnp.float32),
    )
    return (
        weight_grad,
        routed_sum.astype(jnp.bfloat16),
        shared_hidden_sum.astype(jnp.bfloat16),
        shared_sum.astype(jnp.bfloat16),
    )


def solution(mesh):
    finer = Mesh(mesh.devices.reshape(16, 2, mesh.shape["expert"]), ("dp_0", "dp_1", "expert"))
    return jax.shard_map(
        on_device,
        mesh=finer,
        in_specs=(
            P("expert", DP),
            P("expert", None),
            P("expert", None),
            P("expert", None, DP),
            P(),
            P(),
            P("expert", None, None),
            P("expert", None),
            P("expert", DP),
        ),
        out_specs=(P("expert", None, DP), P("expert", DP, None), P("expert", DP), P("expert", DP)),
        check_vma=False,
    )
```

profile of v0, /device:TPU:1, one launch (start us, length us, event | category | flops | bytes accessed | tf_op | source)
XLA Modules:
  0.0 463.4 jit_solution(7973040655364324792)
XLA Ops:
  7.2 2.8 copy.57
  10.0 1.6 copy.58
  11.6 17.9 %all-to-all-start.1 = ((bf16[4,32,32,192]{3,2,0,1:T(8,128)(2,1)}), bf16[4,32,32,192]{3,2,0,1:T(8,128)(2,1)S(1)}, u32[]{:S(2)}, u32[]{:S(2)}) async-start(bf16[4,32,32,192]{3,2,0,1:T(8,128)(2,1)} %copy.58), calls=%async_computation.1 | async-start | bytes 4194304 | tf_op jit(solution)/shard_map/all_to_all | solution.py:71
  29.7 1.2 gather_fusion.1
  31.0 0.1 broadcast_in_dim.70
  31.1 47.8 %all-to-all-done.1 = bf16[4,32,32,192]{3,2,0,1:T(8,128)(2,1)S(1)} async-done(((bf16[4,32,32,192]{3,2,0,1:T(8,128)(2,1)}), bf16[4,32,32,192]{3,2,0,1:T(8,128)(2,1)S(1)}, u32[]{:S(2)}, u32[]{:S(2)}) %all-to-all-start.1) | async-done | bytes 1572896 | tf_op jit(solution)/shard_map/all_to_all | solution.py:71
  78.9 1.3 copy-done.2
  80.3 2.3 gather_fusion.2
  82.5 1.6 broadcast_select_fusion
  84.1 5.8 %all-to-all-start.2 = ((bf16[32,4,32,192]{3,2,1,0:T(8,128)(2,1)}), bf16[32,4,32,192]{3,2,1,0:T(8,128)(2,1)S(1)}, u32[]{:S(2)}, u32[]{:S(2)}) async-start(bf16[32,4,32,192]{3,2,1,0:T(8,128)(2,1)} %broadcast_select_fusion), calls=%async_computation.2 | async-start | bytes 4194304 | tf_op jit(solution)/shard_map/all_to_all | solution.py:87
  90.0 0.1 copy.48
  90.2 0.1 eq.54
  90.3 0.1 reshape.157
  90.4 0.1 copy.51
  90.5 0.2 fusion.7
  90.7 0.7 copy-done.3
  91.5 1.0 broadcast_add_fusion
  92.4 0.7 copy.52
  93.2 0.9 copy.53
  94.1 0.9 mul.37
  95.0 2.0 mul.38
  97.0 0.1 copy.54
  97.3 3.3 gather_fusion
  100.7 1.2 fusion.5
  101.9 3.6 scatter_custom_fusion
  105.5 1.9 reshape.159
  107.4 1.9 copy.55
  109.3 29.9 %all-to-all-done.2 = bf16[32,4,32,192]{3,2,1,0:T(8,128)(2,1)S(1)} async-done(((bf16[32,4,32,192]{3,2,1,0:T(8,128)(2,1)}), bf16[32,4,32,192]{3,2,1,0:T(8,128)(2,1)S(1)}, u32[]{:S(2)}, u32[]{:S(2)}) %all-to-all-start.2) | async-done | bytes 1572896 | tf_op jit(solution)/shard_map/all_to_all | solution.py:87
  139.2 5.7 %all-to-all-start = ((bf16[32,4,5,192]{3,1,2,0:T(4,128)(2,1)}), bf16[32,4,5,192]{3,1,2,0:T(4,128)(2,1)}, u32[]{:S(2)}, u32[]{:S(2)}) async-start(bf16[32,4,5,192]{3,1,2,0:T(4,128)(2,1)} %copy.55), calls=%async_computation | async-start | bytes 655360 | tf_op jit(solution)/shard_map/all_to_all | solution.py:88
  144.9 1.8 copy.59
  146.8 11.2 %all-to-all-done = bf16[32,4,5,192]{3,1,2,0:T(4,128)(2,1)} async-done(((bf16[32,4,5,192]{3,1,2,0:T(4,128)(2,1)}), bf16[32,4,5,192]{3,1,2,0:T(4,128)(2,1)}, u32[]{:S(2)}, u32[]{:S(2)}) %all-to-all-start) | async-done | bytes 245792 | tf_op jit(solution)/shard_map/all_to_all | solution.py:88
  158.0 1.8 convolution_convert_fusion.1
  159.8 2.1 copy.62
  162.0 21.1 %all_to_all.55 = bf16[32,32,192]{2,1,0:T(8,128)(2,1)S(1)} all-to-all(bf16[32,32,192]{2,1,0:T(8,128)(2,1)S(1)} %broadcast_in_dim.73), channel_id=1, replica_groups=mesh['dp_0'=16,'dp_1'=2,'expert'=32] {'expert'}, dimensions={0} | all-to-all | bytes 786432 | tf_op jit(solution)/shard_map/all_to_all | solution.py:18
  183.1 1.0 convolution_convert_fusion.3
  184.1 0.3 convolution_convert_fusion.2
  184.4 1.0 copy.63
  185.4 5.6 %all-to-all-start.4 = ((bf16[32,32,192]{2,1,0:T(8,128)(2,1)}), bf16[32,32,192]{2,1,0:T(8,128)(2,1)S(1)}, u32[]{:S(2)}, u32[]{:S(2)}) async-start(bf16[32,32,192]{2,1,0:T(8,128)(2,1)} %bitcast.22), calls=%async_computation.6 | async-start | bytes 1048576 | tf_op jit(solution)/shard_map/all_to_all | solution.py:35
  191.1 1.3 dynamic-slice
  192.3 1.3 dynamic-slice.2
  194.9 100.3 %all-reduce.5.cloned.1.call-done = bf16[4,160,1024]{2,0,1:T(4,128)(2,1)} async-done(((bf16[4,160,1024]{2,0,1:T(4,128)(2,1)}), bf16[4,160,1024]{2,0,1:T(4,128)(2,1)}) %all-reduce.5.cloned.1.call-update) | async-done | bytes 1310736
  295.2 1.5 constant_dynamic-slice_fusion.1
  296.8 2.7 fusion
  299.6 0.7 reduce_sum.45
  300.3 66.5 %reduce-scatter.3.cloned.1.call-done = bf16[128,64]{0,1:T(8,128)(2,1)} async-done(((bf16[128,1024]{0,1:T(8,128)(2,1)}), bf16[128,64]{0,1:T(8,128)(2,1)}) %reduce-scatter.3.cloned.1.call-update) | async-done | bytes 16400 | tf_op jit(solution)/shard_map/reduce_scatter | solution.py:41
  366.8 62.0 %all-reduce.7.cloned.1.call-done = bf16[4,10,1024]{2,0,1:T(4,128)(2,1)} async-done(((bf16[4,10,1024]{2,0,1:T(4,128)(2,1)}), bf16[4,10,1024]{2,0,1:T(4,128)(2,1)}) %all-reduce.7.cloned.1.call-update) | async-done | bytes 81936
  428.8 1.4 constant_dynamic-slice_fusion
  430.2 26.6 %reduce-scatter.5.cloned.1.call-done = bf16[128,32]{0,1:T(8,128)(2,1)} async-done(((bf16[128,64]{0,1:T(8,128)(2,1)}), bf16[128,32]{0,1:T(8,128)(2,1)}) %reduce-scatter.5.cloned.1.call-update) | async-done | bytes 8208 | tf_op jit(solution)/shard_map/reduce_scatter | solution.py:41
  (45 shorter events, 0.8 us)
Async XLA Ops:
  7.2 289.7 %copy-start = (bf16[4,160,1024]{2,1,0:T(8,128)(2,1)S(1)}, bf16[4,160,1024]{2,1,0:T(8,128)(2,1)}, u32[]{:S(2)}) copy-start(bf16[4,160,1024]{2,1,0:T(8,128)(2,1)} %param.15) | copy-start | bytes 3932164
  11.6 17.9 %copy-start.9 = (s32[128]{0:T(128)S(1)}, s32[128]{0:T(128)}, u32[]{:S(2)}) copy-start(s32[128]{0:T(128)} %param.14) | copy-start | bytes 1540
  11.6 18.0 %copy-start.10 = (s32[128]{0:T(128)S(1)}, s32[128]{0:T(128)}, u32[]{:S(2)}) copy-start(s32[128]{0:T(128)} %param.13) | copy-start | bytes 1540
  11.6 67.3 %all-to-all-start.1 = ((bf16[4,32,32,192]{3,2,0,1:T(8,128)(2,1)}), bf16[4,32,32,192]{3,2,0,1:T(8,128)(2,1)S(1)}, u32[]{:S(2)}, u32[]{:S(2)}) async-start(bf16[4,32,32,192]{3,2,0,1:T(8,128)(2,1)} %copy.58), calls=%async_computation.1 | async-start | bytes 4194304 | tf_op jit(solution)/shard_map/all_to_all | solution.py:71
  78.9 1.3 copy-start.2
  84.1 5.8 %copy-start.7 = (s32[128,4]{0,1:T(4,128)S(1)}, s32[128,4]{0,1:T(4,128)}, u32[]{:S(2)}) copy-start(s32[128,4]{0,1:T(4,128)} %param.11) | copy-start | bytes 6148
  84.1 55.0 %all-to-all-start.2 = ((bf16[32,4,32,192]{3,2,1,0:T(8,128)(2,1)}), bf16[32,4,32,192]{3,2,1,0:T(8,128)(2,1)S(1)}, u32[]{:S(2)}, u32[]{:S(2)}) async-start(bf16[32,4,32,192]{3,2,1,0:T(8,128)(2,1)} %broadcast_select_fusion), calls=%async_computation.2 | async-start | bytes 4194304 | tf_op jit(solution)/shard_map/all_to_all | solution.py:87
  89.9 7.0 %copy-start.8 = (f32[128,4]{0,1:T(4,128)S(1)}, f32[128,4]{0,1:T(4,128)}, u32[]{:S(2)}) copy-start(f32[128,4]{0,1:T(4,128)} %param.10) | copy-start | bytes 6148
  90.7 0.7 copy-start.3
  139.2 5.7 %copy-start.1 = (bf16[32,4,32,192]{3,2,1,0:T(8,128)(2,1)}, bf16[32,4,32,192]{3,2,1,0:T(8,128)(2,1)S(1)}, u32[]{:S(2)}) copy-start(bf16[32,4,32,192]{3,2,1,0:T(8,128)(2,1)S(1)} %all-to-all-done.2) | copy-start | bytes 4718596
  139.2 18.8 %all-to-all-start = ((bf16[32,4,5,192]{3,1,2,0:T(4,128)(2,1)}), bf16[32,4,5,192]{3,1,2,0:T(4,128)(2,1)}, u32[]{:S(2)}, u32[]{:S(2)}) async-start(bf16[32,4,5,192]{3,1,2,0:T(4,128)(2,1)} %copy.55), calls=%async_computation | async-start | bytes 655360 | tf_op jit(solution)/shard_map/all_to_all | solution.py:88
  144.9 150.3 %all-reduce.5.cloned.1.call-start = ((), (), s32[]{:S(2)}) async-start(), calls=%async_computation.9 | async-start | bytes 2621440
  159.8 2.2 copy-start.6
  161.9 21.2 %copy-start.4 = (bf16[128,192]{0,1:T(8,128)(2,1)S(1)}, bf16[128,192]{0,1:T(8,128)(2,1)}, u32[]{:S(2)}) copy-start(bf16[128,192]{0,1:T(8,128)(2,1)} %param.9) | copy-start | bytes 147460
  161.9 22.2 %copy-start.5 = (bf16[128,1024]{1,0:T(8,128)(2,1)S(1)}, bf16[128,1024]{1,0:T(8,128)(2,1)}, u32[]{:S(2)}) copy-start(bf16[128,1024]{1,0:T(8,128)(2,1)} %param.16) | copy-start | bytes 786436
  161.9 204.9 %reduce-scatter.3.cloned.1.call-start = ((), (), s32[]{:S(2)}) async-start(), calls=%async_computation.7 | async-start | bytes 278528 | tf_op jit(solution)/shard_map/reduce_scatter | solution.py:41
  185.4 114.2 %all-to-all-start.4 = ((bf16[32,32,192]{2,1,0:T(8,128)(2,1)}), bf16[32,32,192]{2,1,0:T(8,128)(2,1)S(1)}, u32[]{:S(2)}, u32[]{:S(2)}) async-start(bf16[32,32,192]{2,1,0:T(8,128)(2,1)} %bitcast.22), calls=%async_computation.6 | async-start | bytes 1048576 | tf_op jit(solution)/shard_map/all_to_all | solution.py:35
  191.0 237.8 %all-reduce.7.cloned.1.call-start = ((), (), s32[]{:S(2)}) async-start(), calls=%async_computation.10 | async-start | bytes 163840
  296.8 160.0 %reduce-scatter.5.cloned.1.call-start = ((), (), s32[]{:S(2)}) async-start(), calls=%async_computation.8 | async-start | bytes 24576 | tf_op jit(solution)/shard_map/reduce_scatter | solution.py:41
Sparse Core Ops, SparseCore 0:
  162.0 133.1 all-reduce.4
  298.6 68.1 reduce-scatter.2
  370.2 58.5 all-reduce.6
  432.5 24.2 reduce-scatter.4
where the time goes:
time: 465 us; the launch traced here: 463 us
  waiting for transfers between devices  344 us (74%)
  starting transfers between devices  35.1 us (8%)
  local copies, waits for them, and re-layouts  33.1 us (7%)
  blocking collectives  21.1 us (5%)
  between operations  15.4 us (3%)
  other arithmetic  8.56 us (2%)
  matrix products  5.8 us (1%)
    unnamed x6, waiting for transfers between devices  162 us
    reduce_scatter x2, waiting for transfers between devices, sum_by_axis(): array = lax.psum_scatter(array, axis, scatter_dimension=dim, tiled=True)  93.1 us
    all_to_all x1, waiting for transfers between devices, on_device(): lax.all_to_all(pieces, 'expert', split_axis=1, concat_axis=0, tiled=True)  47.8 us
    all_to_all x1, waiting for transfers between devices, on_device(): lax.all_to_all(ordered, 'expert', split_axis=0, concat_axis=2, tiled=True)  29.9 us
    all_to_all x1, blocking collectives, from_everyone(): lax.all_to_all(jnp.broadcast_to(array[None], (length, *array.shape)), axi...  21.1 us
    all_to_all x1, starting transfers between devices, on_device(): lax.all_to_all(pieces, 'expert', split_axis=1, concat_axis=0, tiled=True)  17.9 us
    all_to_all x1, waiting for transfers between devices, on_device(): lax.all_to_all(outgoing, 'expert', split_axis=0, concat_axis=2, tiled=True)  11.2 us
    unnamed x30, local copies, waits for them, and re-layouts  10.7 us
  transfers between devices with their start and end apart: 8, of which 7 were waited for; matrix products, arithmetic and copies ran while one was open for 7% of the time, Pallas kernels for 0%

commit v1 on v0

v1 whole, which is shorter than its diff:
```python
import jax
import jax.numpy as jnp
from jax import lax
from jax.experimental import pallas as pl
from jax.experimental.pallas import tpu as pltpu
from jax.sharding import Mesh
from jax.sharding import PartitionSpec as P

F32, BF16, I32 = jnp.float32, jnp.bfloat16, jnp.int32
INTERPRET = False

MESSAGE = 168


def iota(shape, dim):
    return lax.broadcasted_iota(I32, shape, dim)


def dot(a, b, a_dim=1, b_dim=0):
    return lax.dot_general(a, b, (((a_dim,), (b_dim,)), ((), ())), preferred_element_type=F32)


def call(body, out, *args, flops=0):
    outs = out if isinstance(out, tuple) else (out,)
    moved = sum(x.size * x.dtype.itemsize for x in (*args, *outs))
    return pl.pallas_call(
        body,
        out_shape=out,
        interpret=INTERPRET,
        cost_estimate=pl.CostEstimate(flops=flops, bytes_accessed=moved, transcendentals=0),
    )(*args)


def tails(grad):
    low = grad[128:192, :]
    none = jnp.zeros((64, 128), BF16)
    return jnp.concatenate([low, none], axis=0), jnp.concatenate([none, low], axis=0)


def pack_body(grad_ref, gate_ref, routing_ref, old_ref, new_ref, hidden_ref, weight_ref, out_ref):
    grad = grad_ref[...]
    first, last = tails(grad)
    head = grad[0:128, :]
    wide = (32, 24, 128)
    flat = (768, 128)
    row, lane = iota(wide, 1), iota(wide, 2)
    slot = iota(wide, 0) * 4 + lax.bitwise_and(row, 3)
    pick = jnp.where(lane == slot, 1.0, 0.0).astype(F32).reshape(flat).astype(BF16)
    rank_of_row = lax.shift_right_logical(row, 2).astype(F32).reshape(flat)
    before = jnp.where(iota((128, 128), 0) < iota((128, 128), 1), 1.0, 0.0).astype(BF16)
    routing = routing_ref[...].astype(F32)
    gates = gate_ref[...]

    def rows_for(listing_ref):
        listing = jnp.broadcast_to(listing_ref[...].astype(F32), (128, 128)).astype(BF16)
        expert = dot(pick, listing, 1, 1)
        named = jnp.zeros(flat, F32)
        gate = jnp.zeros(flat, F32)
        for k in range(4):
            match = expert == routing[k : k + 1, :]
            named = jnp.where(match, 1.0, named)
            gate = jnp.where(match, gates[k : k + 1, :], gate)
        rank = dot(named.astype(BF16), before)
        chosen = jnp.logical_and(named > 0.5, rank == rank_of_row)
        select = jnp.where(chosen, 1.0, 0.0).astype(BF16)
        scale = jnp.sum(jnp.where(chosen, gate, 0.0), axis=1, keepdims=True)
        return select, scale

    old_select, old_scale = rows_for(old_ref)
    new_select, new_scale = rows_for(new_ref)
    old_rows = (dot(old_select, head, 1, 1) * old_scale).reshape(wide)
    new_rows = (dot(new_select, head, 1, 1) * new_scale).reshape(wide)
    out_ref[:, 0:48, :] = jnp.concatenate([old_rows, new_rows], axis=1).astype(BF16)
    rest = dot(old_select, first, 1, 1) * old_scale + dot(new_select, last, 1, 1) * new_scale
    out_ref[:, 144:168, :] = rest.reshape(wide).astype(BF16)
    weight = weight_ref[...]
    out_ref[:, 48:80, :] = jnp.broadcast_to(weight[None, :, 0:128], (32, 32, 128))
    both = jnp.concatenate([weight[0:16, 128:192], weight[16:32, 128:192]], axis=1)
    out_ref[:, 80:96, :] = jnp.broadcast_to(both[None], (32, 16, 128))
    hidden = hidden_ref[...]
    out_ref[:, 96:128, :] = dot(hidden, head, 0, 1).reshape(32, 32, 128).astype(BF16)
    low = dot(hidden, first, 0, 1).reshape(32, 32, 128)[:, 0:16]
    high = dot(hidden, last, 0, 1).reshape(32, 32, 128)[:, 16:32]
    out_ref[:, 128:144, :] = (low + high).astype(BF16)


def hidden_body(message_ref, old_weights_ref, grad_ref, out_ref, shared_ref):
    grad = grad_ref[...]
    first, last = tails(grad)
    units = dot(message_ref[:, :, 48:80, :].reshape(1024, 128), grad[0:128, :]).reshape(32, 32, 128)
    pairs = message_ref[:, :, 80:96, :].reshape(512, 128)
    low, high = dot(pairs, first).reshape(32, 16, 128), dot(pairs, last).reshape(32, 16, 128)
    units = units + jnp.concatenate([low, high], axis=1)
    shared_ref[...] = units.reshape(8, 4, 32, 128).astype(BF16)
    weights = old_weights_ref[...].reshape(768, 1024)
    lane = iota((192, 128), 1)
    left = lane < 64
    own = lax.bitwise_and(iota((8, 24, 128), 1), 3).reshape(192, 128)
    wide = (8, 24, 256)
    row = iota(wide, 1) - 20
    where_to = iota(wide, 2) - iota(wide, 0) * 32 - row * 8
    where_to = jnp.where(row >= 0, where_to, -1).reshape(192, 256)

    def step(m, carry):
        heads = message_ref[:, m, 0:48, :].astype(F32)[:, 0:24, :].reshape(192, 128)
        rest = message_ref[:, m, 144:168, :].astype(F32).reshape(192, 128)
        heads_turned = pltpu.roll(heads, 64, 1)
        rest_turned = pltpu.roll(rest, 64, 1)
        blocks = []
        for e in (0, 2):
            blocks.append(jnp.where(own == e, heads, 0.0))
            blocks.append(
                jnp.where(
                    left, jnp.where(own == e, rest, 0.0), jnp.where(own == e + 1, heads_turned, 0.0)
                )
            )
            blocks.append(jnp.where(own == e + 1, jnp.where(left, heads_turned, rest_turned), 0.0))
        total = dot(jnp.concatenate(blocks, axis=1).astype(BF16), weights)
        shared = shared_ref[:, m].reshape(256, 128)
        placed = [
            dot(jnp.where(where_to == j, 1.0, 0.0).astype(BF16), shared) for j in range(8)
        ]
        total = total + jnp.concatenate(placed, axis=1)
        out_ref[m] = total.reshape(8, 24, 1024).astype(BF16)
        return carry

    lax.fori_loop(0, 4, step, 0)


def weight_body(message_ref, saved_ref, out_ref, shared_ref):
    heads = message_ref[:, 0:48, :].astype(F32)[:, 24:48, :].reshape(768, 128)
    rest = message_ref[:, 144:168, :].astype(F32).reshape(768, 128)
    rows = jnp.concatenate([heads, rest], axis=1).astype(BF16)
    line, place = iota((160, 768), 0), iota((160, 768), 1)
    group = lax.shift_right_logical(line * 205, 10)
    start = (line + group) * 4

    def step(e, carry):
        match = jnp.where(place == start + e, 1.0, 0.0).astype(BF16)
        own = dot(match, rows).astype(BF16)
        product = dot(own, saved_ref[e], 0, 0).astype(BF16)
        out_ref[e, 0:128, :] = product[0:128]
        out_ref[e, 128:192, :] = product[192:256]
        return carry

    lax.fori_loop(0, 4, step, 0)
    total = jnp.sum(message_ref[:, 96:144, :].astype(F32), axis=0)
    shared_ref[:, 0:128] = total[0:32].astype(BF16)
    tail = jnp.concatenate([total[32:48, 0:64], pltpu.roll(total[32:48], 64, 1)[:, 0:64]], axis=0)
    shared_ref[:, 128:192] = tail.astype(BF16)


def partial_body(in_ref, out_ref):
    out_ref[...] = jnp.sum(in_ref[...].astype(F32), axis=0).astype(BF16)


def spread_body(in_ref, out_ref, shared_ref):
    total = jnp.sum(in_ref[...].astype(F32), axis=0)
    for c in range(5):
        for h in range(4):
            piece = total[c * 4 : c * 4 + 4]
            at = h * 256
            both = jnp.concatenate([piece[:, at : at + 128], piece[:, at + 128 : at + 256]], axis=0)
            out_ref[c * 4 + h] = both.astype(BF16)
    out_ref[20:32] = jnp.zeros((12, 8, 128), BF16)
    units = [
        total[20 + r : 21 + r, j * 128 : (j + 1) * 128] for r in range(4) for j in range(8)
    ]
    shared_ref[...] = jnp.concatenate(units, axis=0).astype(BF16)


def permute_body(in_ref, old_ref, new_ref, out_ref):
    line, lane = iota((256, 128), 0), iota((256, 128), 1)
    slot = lax.shift_right_logical(line, 3) * 4 + lax.bitwise_and(line, 3)
    pick = jnp.where(lane == slot, 1.0, 0.0)
    wide = jnp.broadcast_to(new_ref[...].astype(F32), (256, 128)).astype(BF16)
    to = dot(pick.astype(BF16), wide, 1, 1)
    mine = jnp.broadcast_to(old_ref[...].astype(F32), (256, 128)).astype(BF16)
    source = dot(mine, pick.astype(BF16), 1, 1)
    side = lax.bitwise_and(iota((256, 256), 0), 4) == lax.bitwise_and(iota((256, 256), 1), 4)
    match = jnp.where(jnp.logical_and(to == source, side), 1.0, 0.0).astype(BF16)
    moved = dot(match, in_ref[...].reshape(256, 128))
    out_ref[...] = moved.reshape(32, 8, 128).astype(BF16)


def gather_body(in_ref, out_ref):
    for c in range(5):
        for h in range(4):
            both = in_ref[c * 4 + h].astype(F32)
            at = h * 256
            out_ref[c, :, at : at + 128] = both[0:4].astype(BF16)
            out_ref[c, :, at + 128 : at + 256] = both[4:8].astype(BF16)


def pack(grad, gates, routing, old, new, hidden, weight):
    out = jax.ShapeDtypeStruct((32, MESSAGE, 128), BF16)
    return call(pack_body, out, grad, gates, routing, old, new, hidden, weight, flops=10**9)


def hidden_terms(message, weights, grad):
    message = message.reshape(8, 4, MESSAGE, 128)
    out = jax.ShapeDtypeStruct((4, 8, 24, 1024), BF16)
    moved = sum(x.size * 2 for x in (message, weights, grad, out))
    return pl.pallas_call(
        hidden_body,
        out_shape=out,
        scratch_shapes=[pltpu.VMEM((8, 4, 32, 128), BF16)],
        interpret=INTERPRET,
        cost_estimate=pl.CostEstimate(flops=2 * 10**9, bytes_accessed=moved, transcendentals=0),
    )(message, weights, grad)


def weight_terms(message, saved):
    out = (
        jax.ShapeDtypeStruct((4, 192, 1024), BF16),
        jax.ShapeDtypeStruct((32, 192), BF16),
    )
    return call(weight_body, out, message, saved, flops=10**9)


def partial_sum(received):
    return call(partial_body, jax.ShapeDtypeStruct(received.shape[1:], BF16), received)


def spread(received):
    out = (jax.ShapeDtypeStruct((32, 8, 128), BF16), jax.ShapeDtypeStruct((32, 128), BF16))
    return call(spread_body, out, received)


def permute(received, old, new):
    return call(permute_body, jax.ShapeDtypeStruct((32, 8, 128), BF16), received, old, new)


def gather(received):
    return call(gather_body, jax.ShapeDtypeStruct((5, 4, 1024), BF16), received)


def exchange(array, axes):
    return lax.all_to_all(array, axes, 0, 0, tiled=True)


def on_device(
    grad_output,
    gate_probs,
    routing,
    old_weights,
    old_slot_expert,
    new_slot_expert,
    saved_hidden,
    shared_hidden,
    shared_weight,
):
    grad = grad_output.T
    old, new = old_slot_expert.reshape(1, 128), new_slot_expert.reshape(1, 128)
    message = pack(grad, gate_probs.T, routing.T, old, new, shared_hidden, shared_weight)
    message = exchange(message, "expert")
    terms = hidden_terms(message, old_weights.swapaxes(1, 2), grad)
    terms = partial_sum(exchange(terms, ("z_lo", "x_hi")))
    weight_grad, shared_weight_grad = weight_terms(message, saved_hidden)
    pieces, shared_hidden_grad = spread(exchange(terms, "z_hi"))
    pieces = permute(exchange(pieces, "expert"), old, new)
    hidden_grad = gather(exchange(pieces, "expert"))
    return (
        weight_grad.swapaxes(1, 2),
        hidden_grad.swapaxes(0, 1),
        shared_hidden_grad.T,
        shared_weight_grad,
    )


def solution(mesh):
    dp = ("z_hi", "z_lo", "x_hi")
    finer = Mesh(mesh.devices.reshape(8, 2, 2, mesh.shape["expert"]), (*dp, "expert"))
    return jax.shard_map(
        on_device,
        mesh=finer,
        in_specs=(
            P("expert", dp),
            P("expert", None),
            P("expert", None),
            P("expert", None, dp),
            P(),
            P(),
            P("expert", None, None),
            P("expert", None),
            P("expert", dp),
        ),
        out_specs=(P("expert", None, dp), P("expert", dp, None), P("expert", dp), P("expert", dp)),
        check_vma=False,
    )
```

time: 465 us -> 161 us (0.35)
  waiting for transfers between devices: 344 us -> 2.61 us
  blocking collectives: 21.1 us -> 129 us
  local copies, waits for them, and re-layouts: 33.1 us -> 0.62 us
  starting transfers between devices: 35.1 us -> 4.7 us
  Pallas kernels: 0 us -> 22.1 us
  between operations: 15.4 us -> 0.65 us
  other arithmetic: 8.56 us -> 0 us
  matrix products: 5.8 us -> 0 us
    unnamed x6 -> x0, waiting for transfers between devices: 162 us -> none
    all_to_all x1 -> x4, blocking collectives: 21.1 us -> 129 us  [exchange(): return lax.all_to_all(array, axes, 0, 0, tiled=True)]
    reduce_scatter x2 -> x0, waiting for transfers between devices: 93.1 us -> none  [sum_by_axis(): array = lax.psum_scatter(array, axis, scatter_dimension=dim, tiled=True)]
    all_to_all x4 -> x1, waiting for transfers between devices: 88.9 us -> 2.61 us  [exchange(): return lax.all_to_all(array, axes, 0, 0, tiled=True)]
    all_to_all x4 -> x1, starting transfers between devices: 35 us -> 4.7 us  [exchange(): return lax.all_to_all(array, axes, 0, 0, tiled=True)]
    pallas_call x0 -> x7, Pallas kernels: none -> 22.1 us  [the longest x6 16.1 us: call(): pl.pallas_call(body, out_shape=out, interpret=INTERPRET, cost_estimate=pl...]
    unnamed x30 -> x2, local copies, waits for them, and re-layouts: 10.7 us -> 0.62 us
    gather x3 -> x0, local copies, waits for them, and re-layouts: 6.85 us -> none  [the longest x1 3.35 us: on_device(): target = jnp.take(new_position, flat_routes) * capacity + ranking]
  transfers between devices with their start and end apart: 8 -> 1, of which waited for: 7 -> 1; matrix products, arithmetic and copies ran while one was open for 7% -> 0% of each run, Pallas kernels for 0% -> 3%
where the time goes in v1:
time: 161 us; the launch traced here: 160 us
  blocking collectives  129 us (80%)
  Pallas kernels  22.1 us (14%)
  starting transfers between devices  4.7 us (3%)
  waiting for transfers between devices  2.61 us (2%)
    all_to_all x4, blocking collectives, exchange(): return lax.all_to_all(array, axes, 0, 0, tiled=True)  129 us
    pallas_call x6, Pallas kernels, call(): pl.pallas_call(body, out_shape=out, interpret=INTERPRET, cost_estimate=pl...  16.1 us
    pallas_call x1, Pallas kernels, hidden_terms(): pl.pallas_call(hidden_body, out_shape=out, scratch_shapes=[pltpu.VMEM((8,...  6.02 us
    all_to_all x1, starting transfers between devices, exchange(): return lax.all_to_all(array, axes, 0, 0, tiled=True)  4.7 us
  transfers between devices with their start and end apart: 1, of which 1 were waited for; matrix products, arithmetic and copies ran while one was open for 0% of the time, Pallas kernels for 3%

profile of v1, /device:TPU:1, one launch (start us, length us, event | category | flops | bytes accessed | tf_op | source)
XLA Modules:
  0.0 159.9 jit_solution(8257356032526363428)
XLA Ops:
  0.6 3.2 %shard_map.120 = bf16[32,168,128]{2,1,0:T(8,128)(2,1)} custom-call(bf16[192,128]{1,0:T(8,128)(2,1)} %bitcast.17, f32[4,128]{1,0:T(4,128)} %bitcast.20, s32[4,128]{1,0:T(4,128)} %bitcast.21, s32[1,128]{1,0:T(1,128)} %bitcast.12, s32[1,128]{1,0:T(1,128)} %bitcast.14, bf16[128,1024]{1,0:T(8,128)(2,1)} %hidden_ref.1, bf16[32,192]{1,0:T(8,128)(2,1)} %weight_ref.1), custom_call_target="tpu_custom_call" | custom-call | flops 1000000000 | bytes 1704960 | tf_op jit(solution)/shard_map/pallas_call | solution.py:26
  3.8 53.8 %all_to_all.25.message_ref = bf16[32,168,128]{2,1,0:T(8,128)(2,1)} all-to-all(bf16[32,168,128]{2,1,0:T(8,128)(2,1)} %shard_map.120), channel_id=1, replica_groups=mesh['z_hi'=8,'z_lo'=2,'x_hi'=2,'expert'=32] {'expert'}, dimensions={0} | all-to-all | bytes 2752512 | tf_op jit(solution)/shard_map/all_to_all | solution.py:239
  57.6 6.0 %shard_map.122 = bf16[4,8,24,1024]{3,2,1,0:T(8,128)(2,1)} custom-call(bf16[8,4,168,128]{3,2,1,0:T(8,128)(2,1)} %bitcast.10, bf16[4,192,1024]{2,1,0:T(8,128)(2,1)} %bitcast.16, bf16[192,128]{1,0:T(8,128)(2,1)} %bitcast.18), custom_call_target="tpu_custom_call" | custom-call | flops 2000000000 | bytes 4571136 | tf_op jit(solution)/shard_map/pallas_call | solution.py:204
  63.6 23.1 %all_to_all.26.in_ref = bf16[4,8,24,1024]{3,2,1,0:T(8,128)(2,1)} all-to-all(bf16[4,8,24,1024]{3,2,1,0:T(8,128)(2,1)} %shard_map.122), channel_id=1, replica_groups=mesh['z_hi'=8,'z_lo'=2,'x_hi'=2,'expert'=32] {'z_lo','x_hi'}, dimensions={0} | all-to-all | bytes 3145728 | tf_op jit(solution)/shard_map/all_to_all | solution.py:239
  86.7 2.3 %shard_map.123 = bf16[8,24,1024]{2,1,0:T(8,128)(2,1)} custom-call(bf16[4,8,24,1024]{3,2,1,0:T(8,128)(2,1)} %all_to_all.26.in_ref), custom_call_target="tpu_custom_call" | custom-call | bytes 1966080 | tf_op jit(solution)/shard_map/pallas_call | solution.py:26
  89.1 29.7 %all_to_all.27.in_ref = bf16[8,24,1024]{2,1,0:T(8,128)(2,1)} all-to-all(bf16[8,24,1024]{2,1,0:T(8,128)(2,1)} %shard_map.123), channel_id=1, replica_groups=mesh['z_hi'=8,'z_lo'=2,'x_hi'=2,'expert'=32] {'z_hi'}, dimensions={0} | all-to-all | bytes 786432 | tf_op jit(solution)/shard_map/all_to_all | solution.py:239
  118.8 1.7 %shard_map.124 = (bf16[32,8,128]{2,1,0:T(8,128)(2,1)}, bf16[32,128]{1,0:T(8,128)(2,1)}) custom-call(bf16[8,24,1024]{2,1,0:T(8,128)(2,1)} %all_to_all.27.in_ref), custom_call_target="tpu_custom_call" | custom-call | bytes 466944 | tf_op jit(solution)/shard_map/pallas_call | solution.py:26
  120.5 22.6 %all_to_all.28.in_ref = bf16[32,8,128]{2,1,0:T(8,128)(2,1)} all-to-all(bf16[32,8,128]{2,1,0:T(8,128)(2,1)} %get-tuple-element.9), channel_id=1, replica_groups=mesh['z_hi'=8,'z_lo'=2,'x_hi'=2,'expert'=32] {'expert'}, dimensions={0} | all-to-all | bytes 131072 | tf_op jit(solution)/shard_map/all_to_all | solution.py:239
  143.1 1.9 %shard_map.125 = bf16[32,8,128]{2,1,0:T(8,128)(2,1)} custom-call(bf16[32,8,128]{2,1,0:T(8,128)(2,1)} %all_to_all.28.in_ref, s32[1,128]{1,0:T(1,128)} %bitcast.13, s32[1,128]{1,0:T(1,128)} %bitcast.15), custom_call_target="tpu_custom_call" | custom-call | bytes 132096 | tf_op jit(solution)/shard_map/pallas_call | solution.py:26
  145.0 4.7 %all-to-all-start.4 = ((bf16[32,8,128]{2,1,0:T(8,128)(2,1)}), bf16[32,8,128]{2,1,0:T(8,128)(2,1)S(1)}, u32[]{:S(2)}, u32[]{:S(2)}) async-start(bf16[32,8,128]{2,1,0:T(8,128)(2,1)} %shard_map.125), calls=%async_computation.4 | async-start | bytes 131072 | tf_op jit(solution)/shard_map/all_to_all | solution.py:239
  149.7 5.6 %shard_map.121 = (bf16[4,192,1024]{2,1,0:T(8,128)(2,1)}, bf16[32,192]{1,0:T(8,128)(2,1)}) custom-call(bf16[32,168,128]{2,1,0:T(8,128)(2,1)} %all_to_all.25.message_ref, bf16[4,160,1024]{2,1,0:T(8,128)(2,1)} %saved_ref.1), custom_call_target="tpu_custom_call" | custom-call | flops 1000000000 | bytes 4272128 | tf_op jit(solution)/shard_map/pallas_call | solution.py:26
  155.2 2.6 %all-to-all-done.4.in_ref = bf16[32,8,128]{2,1,0:T(8,128)(2,1)S(1)} async-done(((bf16[32,8,128]{2,1,0:T(8,128)(2,1)}), bf16[32,8,128]{2,1,0:T(8,128)(2,1)S(1)}, u32[]{:S(2)}, u32[]{:S(2)}) %all-to-all-start.4) | async-done | bytes 65568 | tf_op jit(solution)/shard_map/all_to_all | solution.py:239
  157.8 0.0 copy-start
  157.8 0.6 copy-done
  158.5 1.5 shard_map.126
Async XLA Ops:
  145.0 12.9 %all-to-all-start.4 = ((bf16[32,8,128]{2,1,0:T(8,128)(2,1)}), bf16[32,8,128]{2,1,0:T(8,128)(2,1)S(1)}, u32[]{:S(2)}, u32[]{:S(2)}) async-start(bf16[32,8,128]{2,1,0:T(8,128)(2,1)} %shard_map.125), calls=%async_computation.4 | async-start | bytes 131072 | tf_op jit(solution)/shard_map/all_to_all | solution.py:239
  157.8 0.6 copy-start

commit v2 on v1

v2 whole, which is shorter than its diff:
```python
import functools

import jax
import jax.numpy as jnp
from jax import lax
from jax.experimental import pallas as pl
from jax.experimental.pallas import tpu as pltpu
from jax.sharding import Mesh
from jax.sharding import PartitionSpec as P

F32, BF16, I32 = jnp.float32, jnp.bfloat16, jnp.int32
INTERPRET = False

MESSAGE = 120
DP = ("z_hi", "z_lo", "x_hi")
EXPERT = ("x_lo", "y2", "y1", "y0", "core")


def iota(shape, dim):
    return lax.broadcasted_iota(I32, shape, dim)


def dot(a, b, a_dim=1, b_dim=0):
    return lax.dot_general(a, b, (((a_dim,), (b_dim,)), ((), ())), preferred_element_type=F32)


def call(body, out, *args, flops=0, held=()):
    outs = out if isinstance(out, tuple) else (out,)
    moved = sum(x.size * x.dtype.itemsize for x in (*args, *outs))
    in_vmem, anywhere = pl.BlockSpec(memory_space=pltpu.VMEM), pl.BlockSpec()
    args = [
        pltpu.with_memory_space_constraint(x, pltpu.VMEM) if i in held else x
        for i, x in enumerate(args)
    ]
    return pl.pallas_call(
        body,
        out_shape=out,
        in_specs=[in_vmem if i in held else anywhere for i in range(len(args))],
        interpret=INTERPRET,
        cost_estimate=pl.CostEstimate(flops=flops, bytes_accessed=moved, transcendentals=0),
    )(*args)


def tails(grad):
    low = grad[128:192, :]
    none = jnp.zeros((64, 128), BF16)
    return jnp.concatenate([low, none], axis=0), jnp.concatenate([none, low], axis=0)


def pack_body(grad_ref, gate_ref, routing_ref, old_ref, new_ref, weight_ref, out_ref):
    grad = grad_ref[...]
    first, last = tails(grad)
    head = grad[0:128, :]
    wide = (32, 24, 128)
    flat = (768, 128)
    row, lane = iota(wide, 1), iota(wide, 2)
    slot = iota(wide, 0) * 4 + lax.bitwise_and(row, 3)
    pick = jnp.where(lane == slot, 1.0, 0.0).astype(F32).reshape(flat).astype(BF16)
    rank_of_row = lax.shift_right_logical(row, 2).astype(F32).reshape(flat)
    before = jnp.where(iota((128, 128), 0) < iota((128, 128), 1), 1.0, 0.0).astype(BF16)
    routing = routing_ref[...].astype(F32)
    gates = gate_ref[...]

    def rows_for(listing_ref):
        listing = jnp.broadcast_to(listing_ref[...].astype(F32), (128, 128)).astype(BF16)
        expert = dot(pick, listing, 1, 1)
        named = jnp.zeros(flat, F32)
        gate = jnp.zeros(flat, F32)
        for k in range(4):
            match = expert == routing[k : k + 1, :]
            named = jnp.where(match, 1.0, named)
            gate = jnp.where(match, gates[k : k + 1, :], gate)
        rank = dot(named.astype(BF16), before)
        chosen = jnp.logical_and(named > 0.5, rank == rank_of_row)
        select = jnp.where(chosen, 1.0, 0.0).astype(BF16)
        scale = jnp.sum(jnp.where(chosen, gate, 0.0), axis=1, keepdims=True)
        return select, scale

    old_select, old_scale = rows_for(old_ref)
    new_select, new_scale = rows_for(new_ref)
    old_rows = (dot(old_select, head, 1, 1) * old_scale).reshape(wide)
    new_rows = (dot(new_select, head, 1, 1) * new_scale).reshape(wide)
    out_ref[:, 0:48, :] = jnp.concatenate([old_rows, new_rows], axis=1).astype(BF16)
    rest = dot(old_select, first, 1, 1) * old_scale + dot(new_select, last, 1, 1) * new_scale
    out_ref[:, 96:120, :] = rest.reshape(wide).astype(BF16)
    weight = weight_ref[...]
    out_ref[:, 48:80, :] = jnp.broadcast_to(weight[None, :, 0:128], (32, 32, 128))
    both = jnp.concatenate([weight[0:16, 128:192], weight[16:32, 128:192]], axis=1)
    out_ref[:, 80:96, :] = jnp.broadcast_to(both[None], (32, 16, 128))


def position(axis):
    return lax.axis_index(axis)


def shared_body(hidden_ref, grad_ref, keep_ref, send_ref, terms_ref):
    grad = grad_ref[...]
    first, last = tails(grad)
    hidden = hidden_ref[...]
    terms_ref[:, :, 0:32, :] = dot(hidden, grad[0:128, :], 0, 1).reshape(16, 2, 32, 128)
    low = dot(hidden, first, 0, 1).reshape(32, 32, 128)[:, 0:16]
    high = dot(hidden, last, 0, 1).reshape(32, 32, 128)[:, 16:32]
    terms_ref[:, :, 32:48, :] = (low + high).reshape(16, 2, 16, 128)
    mine = position("core")
    keep_ref[...] = terms_ref[:, mine]
    send_ref[...] = terms_ref[:, 1 - mine].astype(BF16)


def halve_body(axis, keep_ref, received_ref, next_ref, send_ref):
    mine = position(axis)
    other = 1 - mine
    next_ref[...] = keep_ref[:, mine] + received_ref[:, mine].astype(F32)
    send_ref[...] = (keep_ref[:, other] + received_ref[:, other].astype(F32)).astype(BF16)


def finish_body(keep_ref, received_ref, out_ref):
    total = keep_ref[0] + received_ref[0].astype(F32)
    out_ref[:, 0:128] = total[0:32].astype(BF16)
    tail = jnp.concatenate([total[32:48, 0:64], pltpu.roll(total[32:48], 64, 1)[:, 0:64]], axis=0)
    out_ref[:, 128:192] = tail.astype(BF16)


def hidden_body(message_ref, old_weights_ref, grad_ref, out_ref, new_ref):
    m = pl.program_id(0)

    def part(start, stop):
        return jnp.stack([message_ref[z * 4 + m, start:stop, :] for z in range(8)])

    grad = grad_ref[...]
    first, last = tails(grad)
    lane = iota((192, 128), 1)
    left = lane < 64
    own = lax.bitwise_and(iota((8, 24, 128), 1), 3).reshape(192, 128)
    wide = (8, 24, 256)
    row = iota(wide, 1) - 20
    where_to = iota(wide, 2) - iota(wide, 0) * 32 - row * 8
    where_to = jnp.where(row >= 0, where_to, -1).reshape(192, 256)
    heads = part(0, 48).astype(F32)
    rest = part(96, 120).astype(F32)
    new_ref[:, 0] = jnp.concatenate([heads[:, 24:48], rest], axis=1).astype(BF16)
    heads = heads[:, 0:24].reshape(192, 128)
    rest = rest.reshape(192, 128)
    heads_turned = pltpu.roll(heads, 64, 1)
    rest_turned = pltpu.roll(rest, 64, 1)
    blocks = []
    for e in (0, 2):
        blocks.append(jnp.where(own == e, heads, 0.0))
        blocks.append(
            jnp.where(
                left, jnp.where(own == e, rest, 0.0), jnp.where(own == e + 1, heads_turned, 0.0)
            )
        )
        blocks.append(jnp.where(own == e + 1, jnp.where(left, heads_turned, rest_turned), 0.0))
    rows = jnp.concatenate(blocks, axis=1).astype(BF16)
    total = dot(rows, old_weights_ref[...].reshape(768, 1024))
    units = dot(part(48, 80).reshape(256, 128), grad[0:128, :]).reshape(8, 32, 128)
    pairs = part(80, 96).reshape(128, 128)
    low, high = dot(pairs, first).reshape(8, 16, 128), dot(pairs, last).reshape(8, 16, 128)
    units = units + jnp.concatenate([low, high], axis=1)
    shared = units.reshape(256, 128).astype(BF16)
    placed = [dot(jnp.where(where_to == j, 1.0, 0.0).astype(BF16), shared) for j in range(8)]
    total = total + jnp.concatenate(placed, axis=1)
    out_ref[0] = total.reshape(8, 24, 1024).astype(BF16)


def weight_body(rows_ref, saved_ref, out_ref):
    rows = rows_ref[...].astype(F32)
    heads = rows[:, 0:24].reshape(768, 128)
    rest = rows[:, 24:48].reshape(768, 128)
    rows = jnp.concatenate([heads, rest], axis=1).astype(BF16)
    line, place = iota((160, 768), 0), iota((160, 768), 1)
    group = lax.shift_right_logical(line * 205, 10)
    start = (line + group) * 4

    def step(e, carry):
        match = jnp.where(place == start + e, 1.0, 0.0).astype(BF16)
        own = dot(match, rows).astype(BF16)
        product = dot(own, saved_ref[e], 0, 0).astype(BF16)
        out_ref[e, 0:128, :] = product[0:128]
        out_ref[e, 128:192, :] = product[192:256]
        return carry

    lax.fori_loop(0, 4, step, 0)


def spread_body(in_ref, out_ref, shared_ref):
    total = jnp.sum(in_ref[...].astype(F32), axis=0)
    for c in range(5):
        for h in range(4):
            piece = total[c * 4 : c * 4 + 4]
            at = h * 256
            both = jnp.concatenate([piece[:, at : at + 128], piece[:, at + 128 : at + 256]], axis=0)
            out_ref[c * 4 + h] = both.astype(BF16)
    out_ref[20:32] = jnp.zeros((12, 8, 128), BF16)
    units = [
        total[20 + r : 21 + r, j * 128 : (j + 1) * 128] for r in range(4) for j in range(8)
    ]
    shared_ref[...] = jnp.concatenate(units, axis=0).astype(BF16)


def match_body(old_ref, new_ref, out_ref):
    line, lane = iota((256, 128), 0), iota((256, 128), 1)
    slot = lax.shift_right_logical(line, 3) * 4 + lax.bitwise_and(line, 3)
    pick = jnp.where(lane == slot, 1.0, 0.0)
    wide = jnp.broadcast_to(new_ref[...].astype(F32), (256, 128)).astype(BF16)
    to = dot(pick.astype(BF16), wide, 1, 1)
    mine = jnp.broadcast_to(old_ref[...].astype(F32), (256, 128)).astype(BF16)
    source = dot(mine, pick.astype(BF16), 1, 1)
    side = lax.bitwise_and(iota((256, 256), 0), 4) == lax.bitwise_and(iota((256, 256), 1), 4)
    out_ref[...] = jnp.where(jnp.logical_and(to == source, side), 1.0, 0.0).astype(BF16)


def permute_body(in_ref, match_ref, out_ref):
    moved = dot(match_ref[...], in_ref[...].reshape(256, 128))
    out_ref[...] = moved.reshape(32, 8, 128).astype(BF16)


def shaped(dtype, *shape):
    return jax.ShapeDtypeStruct(shape, dtype)


def pack(grad, gates, routing, old, new, weight):
    out = shaped(BF16, 32, MESSAGE, 128)
    return call(pack_body, out, grad, gates, routing, old, new, weight, flops=10**9)


def hidden_terms(message, weights, grad):
    out = (shaped(BF16, 4, 8, 24, 1024), shaped(BF16, 8, 4, 48, 128))
    moved = sum(x.size * 2 for x in (message, weights, grad, *out))
    return pl.pallas_call(
        hidden_body,
        grid=(4,),
        in_specs=[pl.BlockSpec(memory_space=pltpu.VMEM)] * 3,
        out_specs=(
            pl.BlockSpec((1, 8, 24, 1024), lambda m: (m, 0, 0, 0)),
            pl.BlockSpec((8, 1, 48, 128), lambda m: (0, m, 0, 0)),
        ),
        out_shape=out,
        interpret=INTERPRET,
        compiler_params=pltpu.CompilerParams(vmem_limit_bytes=40 << 20),
        cost_estimate=pl.CostEstimate(flops=2 * 10**9, bytes_accessed=moved, transcendentals=0),
    )(*(pltpu.with_memory_space_constraint(x, pltpu.VMEM) for x in (message, weights, grad)))


def weight_terms(rows, saved):
    out = shaped(BF16, 4, 192, 1024)
    return call(weight_body, out, rows.reshape(32, 48, 128), saved, flops=10**9)


def partial_sum(received):
    return jnp.sum(received.astype(F32), axis=0).astype(BF16)


def spread(received):
    return call(spread_body, (shaped(BF16, 32, 8, 128), shaped(BF16, 32, 128)), received, held=(0,))


def permute(received, match):
    return call(permute_body, shaped(BF16, 32, 8, 128), received, match, held=(0,))


def gather(received):
    pieces = received[0:20].reshape(5, 4, 2, 4, 128)
    return jnp.transpose(pieces, (0, 3, 1, 2, 4)).reshape(5, 4, 1024)


def exchange(array, axes):
    return lax.all_to_all(array, axes, 0, 0, tiled=True)


def swap(array, axis):
    return lax.ppermute(array, axis, [(0, 1), (1, 0)])


def shared_terms(hidden, grad):
    out = (shaped(F32, 16, 48, 128), shaped(BF16, 16, 48, 128))
    return pl.pallas_call(
        shared_body,
        out_shape=out,
        scratch_shapes=[pltpu.VMEM((16, 2, 48, 128), F32)],
        interpret=INTERPRET,
        cost_estimate=pl.CostEstimate(flops=10**8, bytes_accessed=1 << 20, transcendentals=0),
    )(hidden, grad)


def halve(axis, above, below, keep, received):
    whole = (above, 2, below * 48, 128)
    half = (above, below * 48, 128)
    return call(
        functools.partial(halve_body, axis),
        (shaped(F32, *half), shaped(BF16, *half)),
        keep.reshape(whole),
        received.reshape(whole),
        held=(1,),
    )


def shared_weight_sum(hidden, grad):
    keep, send = shared_terms(hidden, grad)
    last = "core"
    for axis, above, below in (("x_lo", 1, 8), ("y0", 4, 1), ("y1", 2, 1), ("y2", 1, 1)):
        send = swap(send, last)
        keep, send = halve(axis, above, below, keep, send)
        last = axis
    send = swap(send, last)
    return call(finish_body, shaped(BF16, 32, 192), keep, send, held=(1,))


def on_device(
    grad_output,
    gate_probs,
    routing,
    old_weights,
    old_slot_expert,
    new_slot_expert,
    saved_hidden,
    shared_hidden,
    shared_weight,
):
    grad = grad_output.T
    old, new = old_slot_expert.reshape(1, 128), new_slot_expert.reshape(1, 128)
    message = pack(grad, gate_probs.T, routing.T, old, new, shared_weight)
    message = exchange(message, EXPERT)
    shared_weight_grad = shared_weight_sum(shared_hidden, grad)
    match = call(match_body, shaped(BF16, 256, 256), old, new, flops=10**7)
    terms, new_rows = hidden_terms(message, old_weights.swapaxes(1, 2), grad)
    terms = exchange(terms, ("z_lo", "x_hi"))
    terms = partial_sum(terms)
    terms = exchange(terms, "z_hi")
    pieces, shared_hidden_grad = spread(terms)
    pieces = exchange(pieces, EXPERT)
    pieces = permute(pieces, match)
    weight_grad = weight_terms(new_rows, saved_hidden)
    pieces = exchange(pieces, EXPERT)
    hidden_grad = gather(pieces)
    return (
        weight_grad.swapaxes(1, 2),
        hidden_grad.swapaxes(0, 1),
        shared_hidden_grad.T,
        shared_weight_grad,
    )


def solution(mesh):
    finer = Mesh(mesh.devices.reshape(8, *(2,) * 7), (*DP, *EXPERT))
    return jax.shard_map(
        on_device,
        mesh=finer,
        in_specs=(
            P(EXPERT, DP),
            P(EXPERT, None),
            P(EXPERT, None),
            P(EXPERT, None, DP),
            P(),
            P(),
            P(EXPERT, None, None),
            P(EXPERT, None),
            P(EXPERT, DP),
        ),
        out_specs=(P(EXPERT, None, DP), P(EXPERT, DP, None), P(EXPERT, DP), P(EXPERT, DP)),
        check_vma=False,
    )
```

time: 161 us -> 161 us (level); the launches traced: 160 us -> 158 us
  blocking collectives: 129 us -> 63.9 us
  starting transfers between devices: 4.7 us -> 54.7 us
  waiting for transfers between devices: 2.61 us -> 10.5 us
  Pallas kernels: 22.1 us -> 25.4 us
    all_to_all x4 -> x2, blocking collectives: 129 us -> 63.9 us  [exchange(): return lax.all_to_all(array, axes, 0, 0, tiled=True)]
    all_to_all x1 -> x3, starting transfers between devices: 4.7 us -> 31.7 us  [exchange(): return lax.all_to_all(array, axes, 0, 0, tiled=True)]
    ppermute x0 -> x5, starting transfers between devices: none -> 23 us  [swap(): return lax.ppermute(array, axis, [(0, 1), (1, 0)])]
    ppermute x0 -> x5, waiting for transfers between devices: none -> 4.72 us  [swap(): return lax.ppermute(array, axis, [(0, 1), (1, 0)])]
    pallas_call x7 -> x12, Pallas kernels: 22.1 us -> 25.4 us  [the longest x10 19.7 us: call(): pl.pallas_call(body, out_shape=out, in_specs=[in_vmem if i in held else a...]
    all_to_all x1 -> x3, waiting for transfers between devices: 2.61 us -> 5.82 us  [exchange(): return lax.all_to_all(array, axes, 0, 0, tiled=True)]
  transfers between devices with their start and end apart: 1 -> 8, of which waited for: 1 -> 4; matrix products, arithmetic and copies ran while one was open for 0% -> 0% of each run, Pallas kernels for 3% -> 12%
where the time goes in v2:
time: 161 us; the launch traced here: 158 us
  blocking collectives  63.9 us (40%)
  starting transfers between devices  54.7 us (34%)
  Pallas kernels  25.4 us (16%)
  waiting for transfers between devices  10.5 us (7%)
    all_to_all x2, blocking collectives, exchange(): return lax.all_to_all(array, axes, 0, 0, tiled=True)  63.9 us
    all_to_all x3, starting transfers between devices, exchange(): return lax.all_to_all(array, axes, 0, 0, tiled=True)  31.7 us
    ppermute x5, starting transfers between devices, swap(): return lax.ppermute(array, axis, [(0, 1), (1, 0)])  23 us
    pallas_call x10, Pallas kernels, call(): pl.pallas_call(body, out_shape=out, in_specs=[in_vmem if i in held else a...  19.7 us
    all_to_all x3, waiting for transfers between devices, exchange(): return lax.all_to_all(array, axes, 0, 0, tiled=True)  5.82 us
    ppermute x5, waiting for transfers between devices, swap(): return lax.ppermute(array, axis, [(0, 1), (1, 0)])  4.72 us
    pallas_call x1, Pallas kernels, hidden_terms(): pl.pallas_call(hidden_body, grid=(4,), in_specs=[pl.BlockSpec(memory_spac...  3.37 us
  transfers between devices with their start and end apart: 8, of which 4 were waited for; matrix products, arithmetic and copies ran while one was open for 0% of the time, Pallas kernels for 12%

profile of v2, /device:TPU:1, one launch (start us, length us, event | category | flops | bytes accessed | tf_op | source)
XLA Modules:
  0.0 157.8 jit_solution(7651574794691640355)
XLA Ops:
  0.6 2.8 %shard_map.120 = bf16[32,120,128]{2,1,0:T(8,128)(2,1)} custom-call(bf16[192,128]{1,0:T(8,128)(2,1)} %bitcast.29, f32[4,128]{1,0:T(4,128)} %bitcast.43, s32[4,128]{1,0:T(4,128)} %bitcast.44, s32[1,128]{1,0:T(1,128)} %bitcast.38, s32[1,128]{1,0:T(1,128)} %bitcast.40, bf16[32,192]{1,0:T(8,128)(2,1)} %weight_ref.1), custom_call_target="tpu_custom_call" | custom-call | flops 1000000000 | bytes 1049600 | tf_op jit(solution)/shard_map/pallas_call | solution.py:35
  3.4 0.0 copy-start
  3.4 0.0 copy-start.1
  3.4 42.9 %all_to_all.25.message_ref = bf16[32,120,128]{2,1,0:T(8,128)(2,1)S(1)} all-to-all(bf16[32,120,128]{2,1,0:T(8,128)(2,1)} %shard_map.120), channel_id=1, replica_groups=mesh['z_hi'=8,'z_lo'=2,'x_hi'=2,'x_lo'=2,'y2'=2,'y1'=2,'y0'=2,'core'=2] ..., dimensions={0} | all-to-all | bytes 1966080 | tf_op jit(solution)/shard_map/all_to_all | solution.py:268
  46.3 0.0 copy-done
  46.3 0.0 copy-done.1
  46.3 3.4 %shard_map.121 = (bf16[4,8,24,1024]{3,2,1,0:T(8,128)(2,1)S(1)}, bf16[8,4,48,128]{3,2,1,0:T(8,128)(2,1)S(1)}) custom-call(bf16[32,120,128]{2,1,0:T(8,128)(2,1)S(1)} %all_to_all.25.message_ref, bf16[4,192,1024]{2,1,0:T(8,128)(2,1)S(1)} %bitcast.28, bf16[192,128]{1,0:T(8,128)(2,1)S(1)} %bitcast.31), custom_call_target="tpu_custom_call" | custom-call | flops 2000000000 | bytes 4571136 | tf_op jit(solution)/shard_map/pallas_call | solution.py:230
  49.7 0.0 copy-start.2
  49.7 0.7 copy-done.2
  50.4 21.0 %all_to_all.26 = bf16[4,8,24,1024]{3,2,1,0:T(8,128)(2,1)S(1)} all-to-all(bf16[4,8,24,1024]{3,2,1,0:T(8,128)(2,1)S(1)} %get-tuple-element.19), channel_id=1, replica_groups=mesh['z_hi'=8,'z_lo'=2,'x_hi'=2,'x_lo'=2,'y2'=2,'y1'=2,'y0'=2,'core'=2] ..., dimensions={0} | all-to-all | bytes 3145728 | tf_op jit(solution)/shard_map/all_to_all | solution.py:268
  71.5 1.1 reduce_sum.12
  72.6 12.4 %all-to-all-start.2 = ((bf16[8,24,1024]{2,1,0:T(8,128)(2,1)}), bf16[8,24,1024]{2,1,0:T(8,128)(2,1)S(1)}, u32[]{:S(2)}, u32[]{:S(2)}) async-start(bf16[8,24,1024]{2,1,0:T(8,128)(2,1)} %reduce_sum.12), calls=%async_computation.2 | async-start | bytes 786432 | tf_op jit(solution)/shard_map/all_to_all | solution.py:268
  85.0 2.3 %shard_map.126 = (f32[16,48,128]{2,1,0:T(8,128)}, bf16[16,48,128]{2,1,0:T(8,128)(2,1)}) custom-call(bf16[128,1024]{1,0:T(8,128)(2,1)} %hidden_ref.1, bf16[192,128]{1,0:T(8,128)(2,1)} %bitcast.30), custom_call_target="tpu_custom_call" | custom-call | flops 100000000 | bytes 1048576 | tf_op jit(solution)/shard_map/pallas_call | solution.py:277
  87.4 5.9 %collective-permute-start = (bf16[16,48,128]{2,1,0:T(8,128)(2,1)}, bf16[16,48,128]{2,1,0:T(8,128)(2,1)S(1)}, u32[]{:S(2)}, u32[]{:S(2)}) collective-permute-start(bf16[16,48,128]{2,1,0:T(8,128)(2,1)} %get-tuple-element.23), channel_id=1, source_target_pairs={{0,1},{1,0},{2,3},{3,2},{4,5},{5,4},{6,7},{7,6},{8,9},{9,8},{10,11... | collective-permute-start | bytes 589832 | tf_op jit(solution)/shard_map/ppermute | solution.py:272
  93.2 1.3 collective-permute-done
  94.5 1.7 %shard_map.127 = (f32[1,384,128]{2,1,0:T(8,128)}, bf16[1,384,128]{2,1,0:T(8,128)(2,1)}) custom-call(f32[1,2,384,128]{3,2,1,0:T(8,128)} %bitcast.33, bf16[1,2,384,128]{3,2,1,0:T(8,128)(2,1)S(1)} %bitcast.24), custom_call_target="tpu_custom_call" | custom-call | bytes 884736 | tf_op jit(solution)/shard_map/pallas_call | solution.py:35
  96.2 2.7 %collective-permute-start.1 = (bf16[1,384,128]{2,1,0:T(8,128)(2,1)}, bf16[1,384,128]{2,1,0:T(8,128)(2,1)S(1)}, u32[]{:S(2)}, u32[]{:S(2)}) collective-permute-start(bf16[1,384,128]{2,1,0:T(8,128)(2,1)} %get-tuple-element.25), channel_id=1, source_target_pairs={{0,16},{16,0},{1,17},{17,1},{2,18},{18,2},{3,19},{19,3},{4,20},{20... | collective-permute-start | bytes 294920 | tf_op jit(solution)/shard_map/ppermute | solution.py:272
  98.9 5.8 %all-to-all-done.2.in_ref = bf16[8,24,1024]{2,1,0:T(8,128)(2,1)S(1)} async-done(((bf16[8,24,1024]{2,1,0:T(8,128)(2,1)}), bf16[8,24,1024]{2,1,0:T(8,128)(2,1)S(1)}, u32[]{:S(2)}, u32[]{:S(2)}) %all-to-all-start.2) | async-done | bytes 393248 | tf_op jit(solution)/shard_map/all_to_all | solution.py:268
  104.7 0.7 shard_map.123
  105.4 11.7 %all-to-all-start.3 = ((bf16[32,8,128]{2,1,0:T(8,128)(2,1)}), bf16[32,8,128]{2,1,0:T(8,128)(2,1)S(1)}, u32[]{:S(2)}, u32[]{:S(2)}) async-start(bf16[32,8,128]{2,1,0:T(8,128)(2,1)} %get-tuple-element.20), calls=%async_computation.3 | async-start | bytes 131072 | tf_op jit(solution)/shard_map/all_to_all | solution.py:268
  117.1 0.0 collective-permute-done.1
  117.1 1.6 %shard_map.128 = (f32[4,48,128]{2,1,0:T(8,128)}, bf16[4,48,128]{2,1,0:T(8,128)(2,1)}) custom-call(f32[4,2,48,128]{3,2,1,0:T(8,128)} %bitcast.34, bf16[4,2,48,128]{3,2,1,0:T(8,128)(2,1)S(1)} %bitcast.25), custom_call_target="tpu_custom_call" | custom-call | bytes 442368 | tf_op jit(solution)/shard_map/pallas_call | solution.py:35
  118.7 3.2 %collective-permute-start.2 = (bf16[4,48,128]{2,1,0:T(8,128)(2,1)}, bf16[4,48,128]{2,1,0:T(8,128)(2,1)S(1)}, u32[]{:S(2)}, u32[]{:S(2)}) collective-permute-start(bf16[4,48,128]{2,1,0:T(8,128)(2,1)} %get-tuple-element.27), channel_id=1, source_target_pairs={{0,2},{2,0},{1,3},{3,1},{4,6},{6,4},{5,7},{7,5},{8,10},{10,8},{9,1... | collective-permute-start | bytes 147464 | tf_op jit(solution)/shard_map/ppermute | solution.py:272
  121.9 2.1 %collective-permute-done.2 = bf16[4,48,128]{2,1,0:T(8,128)(2,1)S(1)} collective-permute-done((bf16[4,48,128]{2,1,0:T(8,128)(2,1)}, bf16[4,48,128]{2,1,0:T(8,128)(2,1)S(1)}, u32[]{:S(2)}, u32[]{:S(2)}) %collective-permute-start.2) | collective-permute-done | bytes 49184 | tf_op jit(solution)/shard_map/ppermute | solution.py:272
  124.0 1.5 shard_map.129
  125.5 4.1 %collective-permute-start.3 = (bf16[2,48,128]{2,1,0:T(8,128)(2,1)}, bf16[2,48,128]{2,1,0:T(8,128)(2,1)S(1)}, u32[]{:S(2)}, u32[]{:S(2)}) collective-permute-start(bf16[2,48,128]{2,1,0:T(8,128)(2,1)} %get-tuple-element.29), channel_id=1, source_target_pairs={{0,4},{4,0},{1,5},{5,1},{2,6},{6,2},{3,7},{7,3},{8,12},{12,8},{9,1... | collective-permute-start | bytes 73736 | tf_op jit(solution)/shard_map/ppermute | solution.py:272
  129.6 1.6 shard_map.124.match_ref
  131.2 0.0 all-to-all-done.3.in_ref
  131.2 1.7 %shard_map.125 = bf16[32,8,128]{2,1,0:T(8,128)(2,1)} custom-call(bf16[32,8,128]{2,1,0:T(8,128)(2,1)S(1)} %all-to-all-done.3.in_ref, bf16[256,256]{1,0:T(8,128)(2,1)} %shard_map.124.match_ref), custom_call_target="tpu_custom_call" | custom-call | bytes 262144 | tf_op jit(solution)/shard_map/pallas_call | solution.py:35
  132.9 7.6 %all-to-all-start.4 = ((bf16[32,8,128]{2,1,0:T(8,128)(2,1)}), bf16[32,8,128]{2,1,0:T(8,128)(2,1)S(1)}, u32[]{:S(2)}, u32[]{:S(2)}) async-start(bf16[32,8,128]{2,1,0:T(8,128)(2,1)} %shard_map.125), calls=%async_computation.4 | async-start | bytes 131072 | tf_op jit(solution)/shard_map/all_to_all | solution.py:268
  140.5 0.0 collective-permute-done.3
  140.5 1.4 shard_map.130
  141.9 7.2 %collective-permute-start.4 = (bf16[1,48,128]{2,1,0:T(8,128)(2,1)}, bf16[1,48,128]{2,1,0:T(8,128)(2,1)S(1)}, u32[]{:S(2)}, u32[]{:S(2)}) collective-permute-start(bf16[1,48,128]{2,1,0:T(8,128)(2,1)} %get-tuple-element.31), channel_id=1, source_target_pairs={{0,8},{8,0},{1,9},{9,1},{2,10},{10,2},{3,11},{11,3},{4,12},{12,4},... | collective-permute-start | bytes 36872 | tf_op jit(solution)/shard_map/ppermute | solution.py:272
  149.1 1.4 collective-permute-done.4.received_ref
  150.5 1.4 shard_map.131
  151.9 5.3 %shard_map.122 = bf16[4,192,1024]{2,1,0:T(8,128)(2,1)} custom-call(bf16[32,48,128]{2,1,0:T(8,128)(2,1)} %bitcast.32, bf16[4,160,1024]{2,1,0:T(8,128)(2,1)} %saved_ref.1), custom_call_target="tpu_custom_call" | custom-call | flops 1000000000 | bytes 3276800 | tf_op jit(solution)/shard_map/pallas_call | solution.py:35
  157.1 0.0 all-to-all-done.4
  157.1 0.6 slice.4
Async XLA Ops:
  3.4 42.9 %copy-start = (bf16[4,1024,192]{1,2,0:T(8,128)(2,1)S(1)}, bf16[4,1024,192]{1,2,0:T(8,128)(2,1)}, u32[]{:S(2)}) copy-start(bf16[4,1024,192]{1,2,0:T(8,128)(2,1)} %param.12) | copy-start | bytes 4718596
  3.4 42.9 %copy-start.1 = (bf16[128,192]{0,1:T(8,128)(2,1)S(1)}, bf16[128,192]{0,1:T(8,128)(2,1)}, u32[]{:S(2)}) copy-start(bf16[128,192]{0,1:T(8,128)(2,1)} %param.9) | copy-start | bytes 147460
  49.7 0.8 copy-start.2
  72.6 32.1 %all-to-all-start.2 = ((bf16[8,24,1024]{2,1,0:T(8,128)(2,1)}), bf16[8,24,1024]{2,1,0:T(8,128)(2,1)S(1)}, u32[]{:S(2)}, u32[]{:S(2)}) async-start(bf16[8,24,1024]{2,1,0:T(8,128)(2,1)} %reduce_sum.12), calls=%async_computation.2 | async-start | bytes 786432 | tf_op jit(solution)/shard_map/all_to_all | solution.py:268
  87.4 7.1 %collective-permute-start = (bf16[16,48,128]{2,1,0:T(8,128)(2,1)}, bf16[16,48,128]{2,1,0:T(8,128)(2,1)S(1)}, u32[]{:S(2)}, u32[]{:S(2)}) collective-permute-start(bf16[16,48,128]{2,1,0:T(8,128)(2,1)} %get-tuple-element.23), channel_id=1, source_target_pairs={{0,1},{1,0},{2,3},{3,2},{4,5},{5,4},{6,7},{7,6},{8,9},{9,8},{10,11... | collective-permute-start | bytes 589832 | tf_op jit(solution)/shard_map/ppermute | solution.py:272
  96.2 20.9 %collective-permute-start.1 = (bf16[1,384,128]{2,1,0:T(8,128)(2,1)}, bf16[1,384,128]{2,1,0:T(8,128)(2,1)S(1)}, u32[]{:S(2)}, u32[]{:S(2)}) collective-permute-start(bf16[1,384,128]{2,1,0:T(8,128)(2,1)} %get-tuple-element.25), channel_id=1, source_target_pairs={{0,16},{16,0},{1,17},{17,1},{2,18},{18,2},{3,19},{19,3},{4,20},{20... | collective-permute-start | bytes 294920 | tf_op jit(solution)/shard_map/ppermute | solution.py:272
  105.4 25.8 %all-to-all-start.3 = ((bf16[32,8,128]{2,1,0:T(8,128)(2,1)}), bf16[32,8,128]{2,1,0:T(8,128)(2,1)S(1)}, u32[]{:S(2)}, u32[]{:S(2)}) async-start(bf16[32,8,128]{2,1,0:T(8,128)(2,1)} %get-tuple-element.20), calls=%async_computation.3 | async-start | bytes 131072 | tf_op jit(solution)/shard_map/all_to_all | solution.py:268
  118.7 5.3 %collective-permute-start.2 = (bf16[4,48,128]{2,1,0:T(8,128)(2,1)}, bf16[4,48,128]{2,1,0:T(8,128)(2,1)S(1)}, u32[]{:S(2)}, u32[]{:S(2)}) collective-permute-start(bf16[4,48,128]{2,1,0:T(8,128)(2,1)} %get-tuple-element.27), channel_id=1, source_target_pairs={{0,2},{2,0},{1,3},{3,1},{4,6},{6,4},{5,7},{7,5},{8,10},{10,8},{9,1... | collective-permute-start | bytes 147464 | tf_op jit(solution)/shard_map/ppermute | solution.py:272
  125.5 14.9 %collective-permute-start.3 = (bf16[2,48,128]{2,1,0:T(8,128)(2,1)}, bf16[2,48,128]{2,1,0:T(8,128)(2,1)S(1)}, u32[]{:S(2)}, u32[]{:S(2)}) collective-permute-start(bf16[2,48,128]{2,1,0:T(8,128)(2,1)} %get-tuple-element.29), channel_id=1, source_target_pairs={{0,4},{4,0},{1,5},{5,1},{2,6},{6,2},{3,7},{7,3},{8,12},{12,8},{9,1... | collective-permute-start | bytes 73736 | tf_op jit(solution)/shard_map/ppermute | solution.py:272
  132.9 24.2 %all-to-all-start.4 = ((bf16[32,8,128]{2,1,0:T(8,128)(2,1)}), bf16[32,8,128]{2,1,0:T(8,128)(2,1)S(1)}, u32[]{:S(2)}, u32[]{:S(2)}) async-start(bf16[32,8,128]{2,1,0:T(8,128)(2,1)} %shard_map.125), calls=%async_computation.4 | async-start | bytes 131072 | tf_op jit(solution)/shard_map/all_to_all | solution.py:268
  141.9 8.5 %collective-permute-start.4 = (bf16[1,48,128]{2,1,0:T(8,128)(2,1)}, bf16[1,48,128]{2,1,0:T(8,128)(2,1)S(1)}, u32[]{:S(2)}, u32[]{:S(2)}) collective-permute-start(bf16[1,48,128]{2,1,0:T(8,128)(2,1)} %get-tuple-element.31), channel_id=1, source_target_pairs={{0,8},{8,0},{1,9},{9,1},{2,10},{10,2},{3,11},{11,3},{4,12},{12,4},... | collective-permute-start | bytes 36872 | tf_op jit(solution)/shard_map/ppermute | solution.py:272

commit v3 on v2

--- a/solution.py
+++ b/solution.py
@@ -11,7 +11,8 @@
 F32, BF16, I32 = jnp.float32, jnp.bfloat16, jnp.int32
 INTERPRET = False
 
-MESSAGE = 120
+MESSAGE = 88
+SECOND = 48
 DP = ("z_hi", "z_lo", "x_hi")
 EXPERT = ("x_lo", "y2", "y1", "y0", "core")
 
@@ -47,10 +48,9 @@
     return jnp.concatenate([low, none], axis=0), jnp.concatenate([none, low], axis=0)
 
 
-def pack_body(grad_ref, gate_ref, routing_ref, old_ref, new_ref, weight_ref, out_ref):
+def pack_rows(grad_ref, gate_ref, routing_ref, listing_ref):
     grad = grad_ref[...]
     first, last = tails(grad)
-    head = grad[0:128, :]
     wide = (32, 24, 128)
     flat = (768, 128)
     row, lane = iota(wide, 1), iota(wide, 2)
@@ -60,33 +60,44 @@
     before = jnp.where(iota((128, 128), 0) < iota((128, 128), 1), 1.0, 0.0).astype(BF16)
     routing = routing_ref[...].astype(F32)
     gates = gate_ref[...]
-
-    def rows_for(listing_ref):
-        listing = jnp.broadcast_to(listing_ref[...].astype(F32), (128, 128)).astype(BF16)
-        expert = dot(pick, listing, 1, 1)
-        named = jnp.zeros(flat, F32)
-        gate = jnp.zeros(flat, F32)
-        for k in range(4):
-            match = expert == routing[k : k + 1, :]
-            named = jnp.where(match, 1.0, named)
-            gate = jnp.where(match, gates[k : k + 1, :], gate)
-        rank = dot(named.astype(BF16), before)
-        chosen = jnp.logical_and(named > 0.5, rank == rank_of_row)
-        select = jnp.where(chosen, 1.0, 0.0).astype(BF16)
-        scale = jnp.sum(jnp.where(chosen, gate, 0.0), axis=1, keepdims=True)
-        return select, scale
-
-    old_select, old_scale = rows_for(old_ref)
-    new_select, new_scale = rows_for(new_ref)
-    old_rows = (dot(old_select, head, 1, 1) * old_scale).reshape(wide)
-    new_rows = (dot(new_select, head, 1, 1) * new_scale).reshape(wide)
-    out_ref[:, 0:48, :] = jnp.concatenate([old_rows, new_rows], axis=1).astype(BF16)
-    rest = dot(old_select, first, 1, 1) * old_scale + dot(new_select, last, 1, 1) * new_scale
-    out_ref[:, 96:120, :] = rest.reshape(wide).astype(BF16)
+    listing = jnp.broadcast_to(listing_ref[...].astype(F32), (128, 128)).astype(BF16)
+    expert = dot(pick, listing, 1, 1)
+    named = jnp.zeros(flat, F32)
+    gate = jnp.zeros(flat, F32)
+    for k in range(4):
+        match = expert == routing[k : k + 1, :]
+        named = jnp.where(match, 1.0, named)
+        gate = jnp.where(match, gates[k : k + 1, :], gate)
+    rank = dot(named.astype(BF16), before)
+    chosen = jnp.logical_and(named > 0.5, rank == rank_of_row)
+    select = jnp.where(chosen, 1.0, 0.0).astype(BF16)
+    scale = jnp.sum(jnp.where(chosen, gate, 0.0), axis=1, keepdims=True)
+    heads = (dot(select, grad[0:128, :], 1, 1) * scale).reshape(wide)
+    low = (dot(select, first, 1, 1) * scale).reshape(wide)
+    high = (dot(select, last, 1, 1) * scale).reshape(wide)
+    rest = jnp.concatenate([low[:, 0:8] + high[:, 16:24], low[:, 8:16]], axis=1)
+    return heads.astype(BF16), rest.astype(BF16)
+
+
+def unpack_rest(rest):
+    turned = pltpu.roll(rest[:, 0:8].reshape(-1, 128), 64, 1).reshape(-1, 8, 128)
+    return jnp.concatenate([rest, turned], axis=1)
+
+
+def pack_body(grad_ref, gate_ref, routing_ref, old_ref, weight_ref, out_ref):
+    heads, rest = pack_rows(grad_ref, gate_ref, routing_ref, old_ref)
+    out_ref[:, 0:24, :] = heads
+    out_ref[:, 24:40, :] = rest
     weight = weight_ref[...]
-    out_ref[:, 48:80, :] = jnp.broadcast_to(weight[None, :, 0:128], (32, 32, 128))
+    out_ref[:, 40:72, :] = jnp.broadcast_to(weight[None, :, 0:128], (32, 32, 128))
     both = jnp.concatenate([weight[0:16, 128:192], weight[16:32, 128:192]], axis=1)
-    out_ref[:, 80:96, :] = jnp.broadcast_to(both[None], (32, 16, 128))
+    out_ref[:, 72:88, :] = jnp.broadcast_to(both[None], (32, 16, 128))
+
+
+def pack_new_body(grad_ref, gate_ref, routing_ref, new_ref, out_ref):
+    heads, rest = pack_rows(grad_ref, gate_ref, routing_ref, new_ref)
+    out_ref[:, 0:24, :] = heads
+    out_ref[:, 24:40, :] = rest
 
 
 def position(axis):
@@ -120,7 +131,7 @@
     out_ref[:, 128:192] = tail.astype(BF16)
 
 
-def hidden_body(message_ref, old_weights_ref, grad_ref, out_ref, new_ref):
+def hidden_body(message_ref, old_weights_ref, grad_ref, out_ref):
     m = pl.program_id(0)
 
     def part(start, stop):
@@ -135,11 +146,8 @@
     row = iota(wide, 1) - 20
     where_to = iota(wide, 2) - iota(wide, 0) * 32 - row * 8
     where_to = jnp.where(row >= 0, where_to, -1).reshape(192, 256)
-    heads = part(0, 48).astype(F32)
-    rest = part(96, 120).astype(F32)
-    new_ref[:, 0] = jnp.concatenate([heads[:, 24:48], rest], axis=1).astype(BF16)
-    heads = heads[:, 0:24].reshape(192, 128)
-    rest = rest.reshape(192, 128)
+    heads = part(0, 24).astype(F32).reshape(192, 128)
+    rest = unpack_rest(part(24, 40).astype(F32)).reshape(192, 128)
     heads_turned = pltpu.roll(heads, 64, 1)
     rest_turned = pltpu.roll(rest, 64, 1)
     blocks = []
@@ -153,8 +161,8 @@
         blocks.append(jnp.where(own == e + 1, jnp.where(left, heads_turned, rest_turned), 0.0))
     rows = jnp.concatenate(blocks, axis=1).astype(BF16)
     total = dot(rows, old_weights_ref[...].reshape(768, 1024))
-    units = dot(part(48, 80).reshape(256, 128), grad[0:128, :]).reshape(8, 32, 128)
-    pairs = part(80, 96).reshape(128, 128)
+    units = dot(part(40, 72).reshape(256, 128), grad[0:128, :]).reshape(8, 32, 128)
+    pairs = part(72, 88).reshape(128, 128)
     low, high = dot(pairs, first).reshape(8, 16, 128), dot(pairs, last).reshape(8, 16, 128)
     units = units + jnp.concatenate([low, high], axis=1)
     shared = units.reshape(256, 128).astype(BF16)
@@ -164,9 +172,9 @@
 
 
 def weight_body(rows_ref, saved_ref, out_ref):
-    rows = rows_ref[...].astype(F32)
+    rows = rows_ref[:, 8:48, :].astype(F32)
     heads = rows[:, 0:24].reshape(768, 128)
-    rest = rows[:, 24:48].reshape(768, 128)
+    rest = unpack_rest(rows[:, 24:40]).reshape(768, 128)
     rows = jnp.concatenate([heads, rest], axis=1).astype(BF16)
     line, place = iota((160, 768), 0), iota((160, 768), 1)
     group = lax.shift_right_logical(line * 205, 10)
@@ -176,22 +184,22 @@
         match = jnp.where(place == start + e, 1.0, 0.0).astype(BF16)
         own = dot(match, rows).astype(BF16)
         product = dot(own, saved_ref[e], 0, 0).astype(BF16)
-        out_ref[e, 0:128, :] = product[0:128]
-        out_ref[e, 128:192, :] = product[192:256]
+        out_ref[e] = product[0:192]
         return carry
 
     lax.fori_loop(0, 4, step, 0)
 
 
-def spread_body(in_ref, out_ref, shared_ref):
+def spread_body(in_ref, rows_ref, out_ref, shared_ref):
+    out_ref[:, 8:48, :] = rows_ref[...]
     total = jnp.sum(in_ref[...].astype(F32), axis=0)
     for c in range(5):
         for h in range(4):
             piece = total[c * 4 : c * 4 + 4]
             at = h * 256
             both = jnp.concatenate([piece[:, at : at + 128], piece[:, at + 128 : at + 256]], axis=0)
-            out_ref[c * 4 + h] = both.astype(BF16)
-    out_ref[20:32] = jnp.zeros((12, 8, 128), BF16)
+            out_ref[c * 4 + h, 0:8, :] = both.astype(BF16)
+    out_ref[20:32, 0:8, :] = jnp.zeros((12, 8, 128), BF16)
     units = [
         total[20 + r : 21 + r, j * 128 : (j + 1) * 128] for r in range(4) for j in range(8)
     ]
@@ -211,7 +219,7 @@
 
 
 def permute_body(in_ref, match_ref, out_ref):
-    moved = dot(match_ref[...], in_ref[...].reshape(256, 128))
+    moved = dot(match_ref[...], in_ref[:, 0:8, :].reshape(256, 128))
     out_ref[...] = moved.reshape(32, 8, 128).astype(BF16)
 
 
@@ -219,22 +227,24 @@
     return jax.ShapeDtypeStruct(shape, dtype)
 
 
-def pack(grad, gates, routing, old, new, weight):
+def pack(grad, gates, routing, old, weight):
     out = shaped(BF16, 32, MESSAGE, 128)
-    return call(pack_body, out, grad, gates, routing, old, new, weight, flops=10**9)
+    return call(pack_body, out, grad, gates, routing, old, weight, flops=10**9)
+
+
+def pack_new(grad, gates, routing, new):
+    out = shaped(BF16, 32, SECOND - 8, 128)
+    return call(pack_new_body, out, grad, gates, routing, new, flops=10**9)
 
 
 def hidden_terms(message, weights, grad):
-    out = (shaped(BF16, 4, 8, 24, 1024), shaped(BF16, 8, 4, 48, 128))
-    moved = sum(x.size * 2 for x in (message, weights, grad, *out))
+    out = shaped(BF16, 4, 8, 24, 1024)
+    moved = sum(x.size * 2 for x in (message, weights, grad, out))
     return pl.pallas_call(
         hidden_body,
         grid=(4,),
         in_specs=[pl.BlockSpec(memory_space=pltpu.VMEM)] * 3,
-        out_specs=(
-            pl.BlockSpec((1, 8, 24, 1024), lambda m: (m, 0, 0, 0)),
-            pl.BlockSpec((8, 1, 48, 128), lambda m: (0, m, 0, 0)),
-        ),
+        out_specs=pl.BlockSpec((1, 8, 24, 1024), lambda m: (m, 0, 0, 0)),
         out_shape=out,
         interpret=INTERPRET,
         compiler_params=pltpu.CompilerParams(vmem_limit_bytes=40 << 20),
@@ -244,15 +254,16 @@
 
 def weight_terms(rows, saved):
     out = shaped(BF16, 4, 192, 1024)
-    return call(weight_body, out, rows.reshape(32, 48, 128), saved, flops=10**9)
+    return call(weight_body, out, rows, saved, flops=10**9, held=(0,))
 
 
 def partial_sum(received):
     return jnp.sum(received.astype(F32), axis=0).astype(BF16)
 
 
-def spread(received):
-    return call(spread_body, (shaped(BF16, 32, 8, 128), shaped(BF16, 32, 128)), received, held=(0,))
+def spread(received, rows):
+    out = (shaped(BF16, 32, SECOND, 128), shaped(BF16, 32, 128))
+    return call(spread_body, out, received, rows, held=(0, 1))
 
 
 def permute(received, match):
@@ -319,18 +330,19 @@
 ):
     grad = grad_output.T
     old, new = old_slot_expert.reshape(1, 128), new_slot_expert.reshape(1, 128)
-    message = pack(grad, gate_probs.T, routing.T, old, new, shared_weight)
+    message = pack(grad, gate_probs.T, routing.T, old, shared_weight)
     message = exchange(message, EXPERT)
+    new_rows = pack_new(grad, gate_probs.T, routing.T, new)
     shared_weight_grad = shared_weight_sum(shared_hidden, grad)
     match = call(match_body, shaped(BF16, 256, 256), old, new, flops=10**7)
-    terms, new_rows = hidden_terms(message, old_weights.swapaxes(1, 2), grad)
+    terms = hidden_terms(message, old_weights.swapaxes(1, 2), grad)
     terms = exchange(terms, ("z_lo", "x_hi"))
     terms = partial_sum(terms)
     terms = exchange(terms, "z_hi")
-    pieces, shared_hidden_grad = spread(terms)
-    pieces = exchange(pieces, EXPERT)
-    pieces = permute(pieces, match)
-    weight_grad = weight_terms(new_rows, saved_hidden)
+    second, shared_hidden_grad = spread(terms, new_rows)
+    second = exchange(second, EXPERT)
+    pieces = permute(second, match)
+    weight_grad = weight_terms(second, saved_hidden)
     pieces = exchange(pieces, EXPERT)
     hidden_grad = gather(pieces)
     return (

time: 161 us -> 170 us (1.056)
  waiting for transfers between devices: 10.5 us -> 26.2 us
  blocking collectives: 63.9 us -> 58.9 us
  starting transfers between devices: 54.7 us -> 50.8 us
  Pallas kernels: 25.4 us -> 27.3 us
    all_to_all x3, waiting for transfers between devices: 5.82 us -> 17.5 us  [exchange(): return lax.all_to_all(array, axes, 0, 0, tiled=True)]
    all_to_all x2, blocking collectives: 63.9 us -> 58.9 us  [exchange(): return lax.all_to_all(array, axes, 0, 0, tiled=True)]
    ppermute x5, waiting for transfers between devices: 4.72 us -> 8.66 us  [swap(): return lax.ppermute(array, axis, [(0, 1), (1, 0)])]
    ppermute x5, starting transfers between devices: 23 us -> 19.1 us  [swap(): return lax.ppermute(array, axis, [(0, 1), (1, 0)])]
    pallas_call x10 -> x11, Pallas kernels: 19.7 us -> 21.6 us  [call(): pl.pallas_call(body, out_shape=out, in_specs=[in_vmem if i in held else a...]
  transfers between devices with their start and end apart: 8 -> 8, of which waited for: 4 -> 5; matrix products, arithmetic and copies ran while one was open for 0% -> 0% of each run, Pallas kernels for 12% -> 12%
where the time goes in v3:
time: 170 us; the launch traced here: 167 us
  blocking collectives  58.9 us (35%)
  starting transfers between devices  50.8 us (30%)
  Pallas kernels  27.3 us (16%)
  waiting for transfers between devices  26.2 us (15%)
    all_to_all x2, blocking collectives, exchange(): return lax.all_to_all(array, axes, 0, 0, tiled=True)  58.9 us
    all_to_all x3, starting transfers between devices, exchange(): return lax.all_to_all(array, axes, 0, 0, tiled=True)  31.6 us
    pallas_call x11, Pallas kernels, call(): pl.pallas_call(body, out_shape=out, in_specs=[in_vmem if i in held else a...  21.6 us
    ppermute x5, starting transfers between devices, swap(): return lax.ppermute(array, axis, [(0, 1), (1, 0)])  19.1 us
    all_to_all x3, waiting for transfers between devices, exchange(): return lax.all_to_all(array, axes, 0, 0, tiled=True)  17.5 us
    ppermute x5, waiting for transfers between devices, swap(): return lax.ppermute(array, axis, [(0, 1), (1, 0)])  8.66 us
  transfers between devices with their start and end apart: 8, of which 5 were waited for; matrix products, arithmetic and copies ran while one was open for 0% of the time, Pallas kernels for 12%

profile of v3, /device:TPU:1, one launch (start us, length us, event | category | flops | bytes accessed | tf_op | source)
XLA Modules:
  0.0 166.6 jit_solution(15240322650722396770)
XLA Ops:
  0.6 0.0 copy-start.1
  0.6 0.0 copy-start.2
  0.7 2.5 %shard_map.120 = bf16[32,88,128]{2,1,0:T(8,128)(2,1)} custom-call(bf16[192,128]{1,0:T(8,128)(2,1)} %bitcast.28, f32[4,128]{1,0:T(4,128)} %bitcast.42, s32[4,128]{1,0:T(4,128)} %bitcast.44, s32[1,128]{1,0:T(1,128)} %bitcast.37, bf16[32,192]{1,0:T(8,128)(2,1)} %weight_ref.1), custom_call_target="tpu_custom_call" | custom-call | flops 1000000000 | bytes 786944 | tf_op jit(solution)/shard_map/pallas_call | solution.py:36
  3.1 37.9 %all_to_all.25.message_ref = bf16[32,88,128]{2,1,0:T(8,128)(2,1)S(1)} all-to-all(bf16[32,88,128]{2,1,0:T(8,128)(2,1)} %shard_map.120), channel_id=1, replica_groups=mesh['z_hi'=8,'z_lo'=2,'x_hi'=2,'x_lo'=2,'y2'=2,'y1'=2,'y0'=2,'core'=2] ..., dimensions={0} | all-to-all | bytes 1441792 | tf_op jit(solution)/shard_map/all_to_all | solution.py:279
  41.0 0.0 copy-done.1
  41.0 0.0 copy-done.2
  41.0 3.3 %shard_map.121 = bf16[4,8,24,1024]{3,2,1,0:T(8,128)(2,1)S(1)} custom-call(bf16[32,88,128]{2,1,0:T(8,128)(2,1)S(1)} %all_to_all.25.message_ref, bf16[4,192,1024]{2,1,0:T(8,128)(2,1)S(1)} %bitcast.27, bf16[192,128]{1,0:T(8,128)(2,1)S(1)} %bitcast.31), custom_call_target="tpu_custom_call" | custom-call | flops 2000000000 | bytes 3915776 | tf_op jit(solution)/shard_map/pallas_call | solution.py:243
  44.3 21.0 %all_to_all.26 = bf16[4,8,24,1024]{3,2,1,0:T(8,128)(2,1)S(1)} all-to-all(bf16[4,8,24,1024]{3,2,1,0:T(8,128)(2,1)S(1)} %shard_map.121), channel_id=1, replica_groups=mesh['z_hi'=8,'z_lo'=2,'x_hi'=2,'x_lo'=2,'y2'=2,'y1'=2,'y0'=2,'core'=2] ..., dimensions={0} | all-to-all | bytes 3145728 | tf_op jit(solution)/shard_map/all_to_all | solution.py:279
  65.4 1.1 reduce_sum.12
  66.5 12.3 %all-to-all-start.2 = ((bf16[8,24,1024]{2,1,0:T(8,128)(2,1)}), bf16[8,24,1024]{2,1,0:T(8,128)(2,1)S(1)}, u32[]{:S(2)}, u32[]{:S(2)}) async-start(bf16[8,24,1024]{2,1,0:T(8,128)(2,1)} %reduce_sum.12), calls=%async_computation.2 | async-start | bytes 786432 | tf_op jit(solution)/shard_map/all_to_all | solution.py:279
  78.8 2.2 %shard_map.122.rows_ref = bf16[32,40,128]{2,1,0:T(8,128)(2,1)} custom-call(bf16[192,128]{1,0:T(8,128)(2,1)} %bitcast.29, f32[4,128]{1,0:T(4,128)} %bitcast.43, s32[4,128]{1,0:T(4,128)} %bitcast.45, s32[1,128]{1,0:T(1,128)} %bitcast.39), custom_call_target="tpu_custom_call" | custom-call | flops 1000000000 | bytes 381440 | tf_op jit(solution)/shard_map/pallas_call | solution.py:36
  81.0 17.5 %all-to-all-done.2.in_ref = bf16[8,24,1024]{2,1,0:T(8,128)(2,1)S(1)} async-done(((bf16[8,24,1024]{2,1,0:T(8,128)(2,1)}), bf16[8,24,1024]{2,1,0:T(8,128)(2,1)S(1)}, u32[]{:S(2)}, u32[]{:S(2)}) %all-to-all-start.2) | async-done | bytes 393248 | tf_op jit(solution)/shard_map/all_to_all | solution.py:279
  98.5 0.0 copy-start
  98.5 1.0 copy-done
  99.4 0.8 shard_map.123
  100.3 11.2 %all-to-all-start.3 = ((bf16[32,48,128]{2,1,0:T(8,128)(2,1)}), bf16[32,48,128]{2,1,0:T(8,128)(2,1)S(1)}, u32[]{:S(2)}, u32[]{:S(2)}) async-start(bf16[32,48,128]{2,1,0:T(8,128)(2,1)} %get-tuple-element.16), calls=%async_computation.3 | async-start | bytes 786432 | tf_op jit(solution)/shard_map/all_to_all | solution.py:279
  111.5 2.3 %shard_map.127 = (f32[16,48,128]{2,1,0:T(8,128)}, bf16[16,48,128]{2,1,0:T(8,128)(2,1)}) custom-call(bf16[128,1024]{1,0:T(8,128)(2,1)} %hidden_ref.1, bf16[192,128]{1,0:T(8,128)(2,1)} %bitcast.30), custom_call_target="tpu_custom_call" | custom-call | flops 100000000 | bytes 1048576 | tf_op jit(solution)/shard_map/pallas_call | solution.py:288
  113.8 2.1 %collective-permute-start = (bf16[16,48,128]{2,1,0:T(8,128)(2,1)}, bf16[16,48,128]{2,1,0:T(8,128)(2,1)S(1)}, u32[]{:S(2)}, u32[]{:S(2)}) collective-permute-start(bf16[16,48,128]{2,1,0:T(8,128)(2,1)} %get-tuple-element.19), channel_id=1, source_target_pairs={{0,1},{1,0},{2,3},{3,2},{4,5},{5,4},{6,7},{7,6},{8,9},{9,8},{10,11... | collective-permute-start | bytes 589832 | tf_op jit(solution)/shard_map/ppermute | solution.py:283
  115.9 1.4 collective-permute-done
  117.3 1.7 %shard_map.128 = (f32[1,384,128]{2,1,0:T(8,128)}, bf16[1,384,128]{2,1,0:T(8,128)(2,1)}) custom-call(f32[1,2,384,128]{3,2,1,0:T(8,128)} %bitcast.32, bf16[1,2,384,128]{3,2,1,0:T(8,128)(2,1)S(1)} %bitcast.23), custom_call_target="tpu_custom_call" | custom-call | bytes 884736 | tf_op jit(solution)/shard_map/pallas_call | solution.py:36
  119.1 3.3 %collective-permute-start.1 = (bf16[1,384,128]{2,1,0:T(8,128)(2,1)}, bf16[1,384,128]{2,1,0:T(8,128)(2,1)S(1)}, u32[]{:S(2)}, u32[]{:S(2)}) collective-permute-start(bf16[1,384,128]{2,1,0:T(8,128)(2,1)} %get-tuple-element.21), channel_id=1, source_target_pairs={{0,16},{16,0},{1,17},{17,1},{2,18},{18,2},{3,19},{19,3},{4,20},{20... | collective-permute-start | bytes 294920 | tf_op jit(solution)/shard_map/ppermute | solution.py:283
  122.3 3.6 %collective-permute-done.1 = bf16[1,384,128]{2,1,0:T(8,128)(2,1)S(1)} collective-permute-done((bf16[1,384,128]{2,1,0:T(8,128)(2,1)}, bf16[1,384,128]{2,1,0:T(8,128)(2,1)S(1)}, u32[]{:S(2)}, u32[]{:S(2)}) %collective-permute-start.1) | collective-permute-done | bytes 98336 | tf_op jit(solution)/shard_map/ppermute | solution.py:283
  126.0 1.6 shard_map.129
  127.6 2.8 %collective-permute-start.2 = (bf16[4,48,128]{2,1,0:T(8,128)(2,1)}, bf16[4,48,128]{2,1,0:T(8,128)(2,1)S(1)}, u32[]{:S(2)}, u32[]{:S(2)}) collective-permute-start(bf16[4,48,128]{2,1,0:T(8,128)(2,1)} %get-tuple-element.23), channel_id=1, source_target_pairs={{0,2},{2,0},{1,3},{3,1},{4,6},{6,4},{5,7},{7,5},{8,10},{10,8},{9,1... | collective-permute-start | bytes 147464 | tf_op jit(solution)/shard_map/ppermute | solution.py:283
  130.4 2.2 %collective-permute-done.2 = bf16[4,48,128]{2,1,0:T(8,128)(2,1)S(1)} collective-permute-done((bf16[4,48,128]{2,1,0:T(8,128)(2,1)}, bf16[4,48,128]{2,1,0:T(8,128)(2,1)S(1)}, u32[]{:S(2)}, u32[]{:S(2)}) %collective-permute-start.2) | collective-permute-done | bytes 49184 | tf_op jit(solution)/shard_map/ppermute | solution.py:283
  132.6 1.5 shard_map.130
  134.1 3.8 %collective-permute-start.3 = (bf16[2,48,128]{2,1,0:T(8,128)(2,1)}, bf16[2,48,128]{2,1,0:T(8,128)(2,1)S(1)}, u32[]{:S(2)}, u32[]{:S(2)}) collective-permute-start(bf16[2,48,128]{2,1,0:T(8,128)(2,1)} %get-tuple-element.25), channel_id=1, source_target_pairs={{0,4},{4,0},{1,5},{5,1},{2,6},{6,2},{3,7},{7,3},{8,12},{12,8},{9,1... | collective-permute-start | bytes 73736 | tf_op jit(solution)/shard_map/ppermute | solution.py:283
  137.9 1.6 shard_map.125.match_ref
  139.5 0.0 all-to-all-done.3.rows_ref.in_ref
  139.5 1.7 %shard_map.126 = bf16[32,8,128]{2,1,0:T(8,128)(2,1)} custom-call(bf16[32,48,128]{2,1,0:T(8,128)(2,1)S(1)} %all-to-all-done.3.rows_ref.in_ref, bf16[256,256]{1,0:T(8,128)(2,1)} %shard_map.125.match_ref), custom_call_target="tpu_custom_call" | custom-call | bytes 589824 | tf_op jit(solution)/shard_map/pallas_call | solution.py:36
  141.2 8.2 %all-to-all-start.4 = ((bf16[32,8,128]{2,1,0:T(8,128)(2,1)}), bf16[32,8,128]{2,1,0:T(8,128)(2,1)S(1)}, u32[]{:S(2)}, u32[]{:S(2)}) async-start(bf16[32,8,128]{2,1,0:T(8,128)(2,1)} %shard_map.126), calls=%async_computation.4 | async-start | bytes 131072 | tf_op jit(solution)/shard_map/all_to_all | solution.py:279
  149.4 0.0 collective-permute-done.3
  149.4 1.4 shard_map.131
  150.8 7.2 %collective-permute-start.4 = (bf16[1,48,128]{2,1,0:T(8,128)(2,1)}, bf16[1,48,128]{2,1,0:T(8,128)(2,1)S(1)}, u32[]{:S(2)}, u32[]{:S(2)}) collective-permute-start(bf16[1,48,128]{2,1,0:T(8,128)(2,1)} %get-tuple-element.27), channel_id=1, source_target_pairs={{0,8},{8,0},{1,9},{9,1},{2,10},{10,2},{3,11},{11,3},{4,12},{12,4},... | collective-permute-start | bytes 36872 | tf_op jit(solution)/shard_map/ppermute | solution.py:283
  158.0 1.4 collective-permute-done.4.received_ref
  159.3 1.4 shard_map.132
  160.8 5.2 %shard_map.124 = bf16[4,192,1024]{2,1,0:T(8,128)(2,1)} custom-call(bf16[32,48,128]{2,1,0:T(8,128)(2,1)S(1)} %all-to-all-done.3.rows_ref.in_ref, bf16[4,160,1024]{2,1,0:T(8,128)(2,1)} %saved_ref.1), custom_call_target="tpu_custom_call" | custom-call | flops 1000000000 | bytes 3276800 | tf_op jit(solution)/shard_map/pallas_call | solution.py:36
  166.0 0.0 all-to-all-done.4
  166.0 0.6 slice.4
Async XLA Ops:
  0.6 40.4 %copy-start.1 = (bf16[4,1024,192]{1,2,0:T(8,128)(2,1)S(1)}, bf16[4,1024,192]{1,2,0:T(8,128)(2,1)}, u32[]{:S(2)}) copy-start(bf16[4,1024,192]{1,2,0:T(8,128)(2,1)} %param.12) | copy-start | bytes 4718596
  0.6 40.4 %copy-start.2 = (bf16[128,192]{0,1:T(8,128)(2,1)S(1)}, bf16[128,192]{0,1:T(8,128)(2,1)}, u32[]{:S(2)}) copy-start(bf16[128,192]{0,1:T(8,128)(2,1)} %param.9) | copy-start | bytes 147460
  66.5 32.0 %all-to-all-start.2 = ((bf16[8,24,1024]{2,1,0:T(8,128)(2,1)}), bf16[8,24,1024]{2,1,0:T(8,128)(2,1)S(1)}, u32[]{:S(2)}, u32[]{:S(2)}) async-start(bf16[8,24,1024]{2,1,0:T(8,128)(2,1)} %reduce_sum.12), calls=%async_computation.2 | async-start | bytes 786432 | tf_op jit(solution)/shard_map/all_to_all | solution.py:279
  98.5 1.0 copy-start
  100.3 39.2 %all-to-all-start.3 = ((bf16[32,48,128]{2,1,0:T(8,128)(2,1)}), bf16[32,48,128]{2,1,0:T(8,128)(2,1)S(1)}, u32[]{:S(2)}, u32[]{:S(2)}) async-start(bf16[32,48,128]{2,1,0:T(8,128)(2,1)} %get-tuple-element.16), calls=%async_computation.3 | async-start | bytes 786432 | tf_op jit(solution)/shard_map/all_to_all | solution.py:279
  113.8 3.5 %collective-permute-start = (bf16[16,48,128]{2,1,0:T(8,128)(2,1)}, bf16[16,48,128]{2,1,0:T(8,128)(2,1)S(1)}, u32[]{:S(2)}, u32[]{:S(2)}) collective-permute-start(bf16[16,48,128]{2,1,0:T(8,128)(2,1)} %get-tuple-element.19), channel_id=1, source_target_pairs={{0,1},{1,0},{2,3},{3,2},{4,5},{5,4},{6,7},{7,6},{8,9},{9,8},{10,11... | collective-permute-start | bytes 589832 | tf_op jit(solution)/shard_map/ppermute | solution.py:283
  119.1 6.9 %collective-permute-start.1 = (bf16[1,384,128]{2,1,0:T(8,128)(2,1)}, bf16[1,384,128]{2,1,0:T(8,128)(2,1)S(1)}, u32[]{:S(2)}, u32[]{:S(2)}) collective-permute-start(bf16[1,384,128]{2,1,0:T(8,128)(2,1)} %get-tuple-element.21), channel_id=1, source_target_pairs={{0,16},{16,0},{1,17},{17,1},{2,18},{18,2},{3,19},{19,3},{4,20},{20... | collective-permute-start | bytes 294920 | tf_op jit(solution)/shard_map/ppermute | solution.py:283
  127.6 5.0 %collective-permute-start.2 = (bf16[4,48,128]{2,1,0:T(8,128)(2,1)}, bf16[4,48,128]{2,1,0:T(8,128)(2,1)S(1)}, u32[]{:S(2)}, u32[]{:S(2)}) collective-permute-start(bf16[4,48,128]{2,1,0:T(8,128)(2,1)} %get-tuple-element.23), channel_id=1, source_target_pairs={{0,2},{2,0},{1,3},{3,1},{4,6},{6,4},{5,7},{7,5},{8,10},{10,8},{9,1... | collective-permute-start | bytes 147464 | tf_op jit(solution)/shard_map/ppermute | solution.py:283
  134.1 15.2 %collective-permute-start.3 = (bf16[2,48,128]{2,1,0:T(8,128)(2,1)}, bf16[2,48,128]{2,1,0:T(8,128)(2,1)S(1)}, u32[]{:S(2)}, u32[]{:S(2)}) collective-permute-start(bf16[2,48,128]{2,1,0:T(8,128)(2,1)} %get-tuple-element.25), channel_id=1, source_target_pairs={{0,4},{4,0},{1,5},{5,1},{2,6},{6,2},{3,7},{7,3},{8,12},{12,8},{9,1... | collective-permute-start | bytes 73736 | tf_op jit(solution)/shard_map/ppermute | solution.py:283
  141.2 24.8 %all-to-all-start.4 = ((bf16[32,8,128]{2,1,0:T(8,128)(2,1)}), bf16[32,8,128]{2,1,0:T(8,128)(2,1)S(1)}, u32[]{:S(2)}, u32[]{:S(2)}) async-start(bf16[32,8,128]{2,1,0:T(8,128)(2,1)} %shard_map.126), calls=%async_computation.4 | async-start | bytes 131072 | tf_op jit(solution)/shard_map/all_to_all | solution.py:279
  150.8 8.5 %collective-permute-start.4 = (bf16[1,48,128]{2,1,0:T(8,128)(2,1)}, bf16[1,48,128]{2,1,0:T(8,128)(2,1)S(1)}, u32[]{:S(2)}, u32[]{:S(2)}) collective-permute-start(bf16[1,48,128]{2,1,0:T(8,128)(2,1)} %get-tuple-element.27), channel_id=1, source_target_pairs={{0,8},{8,0},{1,9},{9,1},{2,10},{10,2},{3,11},{11,3},{4,12},{12,4},... | collective-permute-start | bytes 36872 | tf_op jit(solution)/shard_map/ppermute | solution.py:283

commit v4 on v3

--- a/solution.py
+++ b/solution.py
@@ -11,7 +11,7 @@
 F32, BF16, I32 = jnp.float32, jnp.bfloat16, jnp.int32
 INTERPRET = False
 
-MESSAGE = 88
+MESSAGE = 80
 SECOND = 48
 DP = ("z_hi", "z_lo", "x_hi")
 EXPERT = ("x_lo", "y2", "y1", "y0", "core")
@@ -48,7 +48,7 @@
     return jnp.concatenate([low, none], axis=0), jnp.concatenate([none, low], axis=0)
 
 
-def pack_rows(grad_ref, gate_ref, routing_ref, listing_ref):
+def pack_rows(grad_ref, gate_ref, routing_ref, listing_ref, ends=None):
     grad = grad_ref[...]
     first, last = tails(grad)
     wide = (32, 24, 128)
@@ -75,7 +75,14 @@
     heads = (dot(select, grad[0:128, :], 1, 1) * scale).reshape(wide)
     low = (dot(select, first, 1, 1) * scale).reshape(wide)
     high = (dot(select, last, 1, 1) * scale).reshape(wide)
-    rest = jnp.concatenate([low[:, 0:8] + high[:, 16:24], low[:, 8:16]], axis=1)
+    upper = low[:, 8:16]
+    if ends is not None:
+        swapped = jnp.concatenate([ends[4:8], ends[0:4]], axis=1)
+        extra = jnp.concatenate([jnp.zeros((4, 128), F32), swapped], axis=0)
+        heads = jnp.concatenate([heads[:, 0:16], heads[:, 16:24] + extra[None]], axis=1)
+        extra = jnp.concatenate([jnp.zeros((8, 64), F32), ends[8:16]], axis=1)
+        upper = upper + extra[None]
+    rest = jnp.concatenate([low[:, 0:8] + high[:, 16:24], upper], axis=1)
     return heads.astype(BF16), rest.astype(BF16)
 
 
@@ -85,13 +92,14 @@
 
 
 def pack_body(grad_ref, gate_ref, routing_ref, old_ref, weight_ref, out_ref):
-    heads, rest = pack_rows(grad_ref, gate_ref, routing_ref, old_ref)
+    weight = weight_ref[...]
+    ends = weight[:, 128:192].astype(F32)
+    heads, rest = pack_rows(grad_ref, gate_ref, routing_ref, old_ref, ends)
     out_ref[:, 0:24, :] = heads
     out_ref[:, 24:40, :] = rest
-    weight = weight_ref[...]
     out_ref[:, 40:72, :] = jnp.broadcast_to(weight[None, :, 0:128], (32, 32, 128))
-    both = jnp.concatenate([weight[0:16, 128:192], weight[16:32, 128:192]], axis=1)
-    out_ref[:, 72:88, :] = jnp.broadcast_to(both[None], (32, 16, 128))
+    both = jnp.concatenate([ends[16:24], ends[24:32]], axis=1).astype(BF16)
+    out_ref[:, 72:80, :] = jnp.broadcast_to(both[None], (32, 8, 128))
 
 
 def pack_new_body(grad_ref, gate_ref, routing_ref, new_ref, out_ref):
@@ -141,13 +149,17 @@
     first, last = tails(grad)
     lane = iota((192, 128), 1)
     left = lane < 64
-    own = lax.bitwise_and(iota((8, 24, 128), 1), 3).reshape(192, 128)
+    own = iota((8, 24, 128), 1)
+    own = jnp.where(own < 20, lax.bitwise_and(own, 3), 4).reshape(192, 128)
     wide = (8, 24, 256)
     row = iota(wide, 1) - 20
     where_to = iota(wide, 2) - iota(wide, 0) * 32 - row * 8
     where_to = jnp.where(row >= 0, where_to, -1).reshape(192, 256)
-    heads = part(0, 24).astype(F32).reshape(192, 128)
-    rest = unpack_rest(part(24, 40).astype(F32)).reshape(192, 128)
+    heads = part(0, 24).astype(F32)
+    rest = part(24, 40).astype(F32)
+    ends = jnp.concatenate([heads[:, 16:24], rest[:, 8:16], part(72, 80).astype(F32)], axis=1)
+    heads = heads.reshape(192, 128)
+    rest = unpack_rest(rest).reshape(192, 128)
     heads_turned = pltpu.roll(heads, 64, 1)
     rest_turned = pltpu.roll(rest, 64, 1)
     blocks = []
@@ -162,9 +174,10 @@
     rows = jnp.concatenate(blocks, axis=1).astype(BF16)
     total = dot(rows, old_weights_ref[...].reshape(768, 1024))
     units = dot(part(40, 72).reshape(256, 128), grad[0:128, :]).reshape(8, 32, 128)
-    pairs = part(72, 88).reshape(128, 128)
-    low, high = dot(pairs, first).reshape(8, 16, 128), dot(pairs, last).reshape(8, 16, 128)
-    units = units + jnp.concatenate([low, high], axis=1)
+    ends = ends.reshape(192, 128).astype(BF16)
+    low, high = dot(ends, first).reshape(8, 24, 128), dot(ends, last).reshape(8, 24, 128)
+    ends = [high[:, 4:8], low[:, 4:8], high[:, 8:16], low[:, 16:24], high[:, 16:24]]
+    units = units + jnp.concatenate(ends, axis=1)
     shared = units.reshape(256, 128).astype(BF16)
     placed = [dot(jnp.where(where_to == j, 1.0, 0.0).astype(BF16), shared) for j in range(8)]
     total = total + jnp.concatenate(placed, axis=1)
@@ -267,7 +280,7 @@
 
 
 def permute(received, match):
-    return call(permute_body, shaped(BF16, 32, 8, 128), received, match, held=(0,))
+    return call(permute_body, shaped(BF16, 32, 8, 128), received, match, held=(0, 1))
 
 
 def gather(received):

time: 170 us -> 168 us (0.988)
  no operation moved by 1% of the time
where the time goes in v4:
time: 168 us; the launch traced here: 165 us
  blocking collectives  57.9 us (34%)
  starting transfers between devices  50.2 us (30%)
  Pallas kernels  26.5 us (16%)
  waiting for transfers between devices  26.2 us (16%)
  local copies, waits for them, and re-layouts  2.51 us (1%)
    all_to_all x2, blocking collectives, exchange(): return lax.all_to_all(array, axes, 0, 0, tiled=True)  57.9 us
    all_to_all x3, starting transfers between devices, exchange(): return lax.all_to_all(array, axes, 0, 0, tiled=True)  31.1 us
    pallas_call x11, Pallas kernels, call(): pl.pallas_call(body, out_shape=out, in_specs=[in_vmem if i in held else a...  20.8 us
    ppermute x5, starting transfers between devices, swap(): return lax.ppermute(array, axis, [(0, 1), (1, 0)])  19.1 us
    all_to_all x3, waiting for transfers between devices, exchange(): return lax.all_to_all(array, axes, 0, 0, tiled=True)  17.5 us
    ppermute x5, waiting for transfers between devices, swap(): return lax.ppermute(array, axis, [(0, 1), (1, 0)])  8.65 us
    pallas_call x1, Pallas kernels, hidden_terms(): pl.pallas_call(hidden_body, grid=(4,), in_specs=[pl.BlockSpec(memory_spac...  3.41 us
  transfers between devices with their start and end apart: 8, of which 5 were waited for; matrix products, arithmetic and copies ran while one was open for 0% of the time, Pallas kernels for 12%

profile of v4, /device:TPU:1, one launch (start us, length us, event | category | flops | bytes accessed | tf_op | source)
XLA Modules:
  0.0 165.2 jit_solution(5908945193866809709)
XLA Ops:
  0.6 0.0 copy-start.2
  0.6 0.0 copy-start.3
  0.7 2.5 %shard_map.120 = bf16[32,80,128]{2,1,0:T(8,128)(2,1)} custom-call(bf16[192,128]{1,0:T(8,128)(2,1)} %bitcast.28, f32[4,128]{1,0:T(4,128)} %bitcast.42, s32[4,128]{1,0:T(4,128)} %bitcast.44, s32[1,128]{1,0:T(1,128)} %bitcast.37, bf16[32,192]{1,0:T(8,128)(2,1)} %weight_ref.1), custom_call_target="tpu_custom_call" | custom-call | flops 1000000000 | bytes 721408 | tf_op jit(solution)/shard_map/pallas_call | solution.py:36
  3.1 36.7 %all_to_all.25.message_ref = bf16[32,80,128]{2,1,0:T(8,128)(2,1)S(1)} all-to-all(bf16[32,80,128]{2,1,0:T(8,128)(2,1)} %shard_map.120), channel_id=1, replica_groups=mesh['z_hi'=8,'z_lo'=2,'x_hi'=2,'x_lo'=2,'y2'=2,'y1'=2,'y0'=2,'core'=2] ..., dimensions={0} | all-to-all | bytes 1310720 | tf_op jit(solution)/shard_map/all_to_all | solution.py:292
  39.9 0.0 copy-done.2
  39.9 0.0 copy-done.3
  39.9 3.4 %shard_map.121 = bf16[4,8,24,1024]{3,2,1,0:T(8,128)(2,1)S(1)} custom-call(bf16[32,80,128]{2,1,0:T(8,128)(2,1)S(1)} %all_to_all.25.message_ref, bf16[4,192,1024]{2,1,0:T(8,128)(2,1)S(1)} %bitcast.27, bf16[192,128]{1,0:T(8,128)(2,1)S(1)} %bitcast.31), custom_call_target="tpu_custom_call" | custom-call | flops 2000000000 | bytes 3850240 | tf_op jit(solution)/shard_map/pallas_call | solution.py:256
  43.3 21.1 %all_to_all.26 = bf16[4,8,24,1024]{3,2,1,0:T(8,128)(2,1)S(1)} all-to-all(bf16[4,8,24,1024]{3,2,1,0:T(8,128)(2,1)S(1)} %shard_map.121), channel_id=1, replica_groups=mesh['z_hi'=8,'z_lo'=2,'x_hi'=2,'x_lo'=2,'y2'=2,'y1'=2,'y0'=2,'core'=2] ..., dimensions={0} | all-to-all | bytes 3145728 | tf_op jit(solution)/shard_map/all_to_all | solution.py:292
  64.4 1.1 reduce_sum.12
  65.5 12.2 %all-to-all-start.2 = ((bf16[8,24,1024]{2,1,0:T(8,128)(2,1)}), bf16[8,24,1024]{2,1,0:T(8,128)(2,1)S(1)}, u32[]{:S(2)}, u32[]{:S(2)}) async-start(bf16[8,24,1024]{2,1,0:T(8,128)(2,1)} %reduce_sum.12), calls=%async_computation.2 | async-start | bytes 786432 | tf_op jit(solution)/shard_map/all_to_all | solution.py:292
  77.8 2.2 %shard_map.122.rows_ref = bf16[32,40,128]{2,1,0:T(8,128)(2,1)} custom-call(bf16[192,128]{1,0:T(8,128)(2,1)} %bitcast.29, f32[4,128]{1,0:T(4,128)} %bitcast.43, s32[4,128]{1,0:T(4,128)} %bitcast.45, s32[1,128]{1,0:T(1,128)} %bitcast.39), custom_call_target="tpu_custom_call" | custom-call | flops 1000000000 | bytes 381440 | tf_op jit(solution)/shard_map/pallas_call | solution.py:36
  80.0 17.5 %all-to-all-done.2.in_ref = bf16[8,24,1024]{2,1,0:T(8,128)(2,1)S(1)} async-done(((bf16[8,24,1024]{2,1,0:T(8,128)(2,1)}), bf16[8,24,1024]{2,1,0:T(8,128)(2,1)S(1)}, u32[]{:S(2)}, u32[]{:S(2)}) %all-to-all-start.2) | async-done | bytes 393248 | tf_op jit(solution)/shard_map/all_to_all | solution.py:292
  97.5 0.0 copy-start.1
  97.5 1.0 copy-done.1
  98.5 0.8 shard_map.123
  99.3 10.7 %all-to-all-start.3 = ((bf16[32,48,128]{2,1,0:T(8,128)(2,1)}), bf16[32,48,128]{2,1,0:T(8,128)(2,1)S(1)}, u32[]{:S(2)}, u32[]{:S(2)}) async-start(bf16[32,48,128]{2,1,0:T(8,128)(2,1)} %get-tuple-element.16), calls=%async_computation.3 | async-start | bytes 786432 | tf_op jit(solution)/shard_map/all_to_all | solution.py:292
  110.0 2.3 %shard_map.127 = (f32[16,48,128]{2,1,0:T(8,128)}, bf16[16,48,128]{2,1,0:T(8,128)(2,1)}) custom-call(bf16[128,1024]{1,0:T(8,128)(2,1)} %hidden_ref.1, bf16[192,128]{1,0:T(8,128)(2,1)} %bitcast.30), custom_call_target="tpu_custom_call" | custom-call | flops 100000000 | bytes 1048576 | tf_op jit(solution)/shard_map/pallas_call | solution.py:301
  112.4 2.1 %collective-permute-start = (bf16[16,48,128]{2,1,0:T(8,128)(2,1)}, bf16[16,48,128]{2,1,0:T(8,128)(2,1)S(1)}, u32[]{:S(2)}, u32[]{:S(2)}) collective-permute-start(bf16[16,48,128]{2,1,0:T(8,128)(2,1)} %get-tuple-element.19), channel_id=1, source_target_pairs={{0,1},{1,0},{2,3},{3,2},{4,5},{5,4},{6,7},{7,6},{8,9},{9,8},{10,11... | collective-permute-start | bytes 589832 | tf_op jit(solution)/shard_map/ppermute | solution.py:296
  114.5 1.4 collective-permute-done
  115.9 1.7 %shard_map.128 = (f32[1,384,128]{2,1,0:T(8,128)}, bf16[1,384,128]{2,1,0:T(8,128)(2,1)}) custom-call(f32[1,2,384,128]{3,2,1,0:T(8,128)} %bitcast.32, bf16[1,2,384,128]{3,2,1,0:T(8,128)(2,1)S(1)} %bitcast.23), custom_call_target="tpu_custom_call" | custom-call | bytes 884736 | tf_op jit(solution)/shard_map/pallas_call | solution.py:36
  117.6 3.3 %collective-permute-start.1 = (bf16[1,384,128]{2,1,0:T(8,128)(2,1)}, bf16[1,384,128]{2,1,0:T(8,128)(2,1)S(1)}, u32[]{:S(2)}, u32[]{:S(2)}) collective-permute-start(bf16[1,384,128]{2,1,0:T(8,128)(2,1)} %get-tuple-element.21), channel_id=1, source_target_pairs={{0,16},{16,0},{1,17},{17,1},{2,18},{18,2},{3,19},{19,3},{4,20},{20... | collective-permute-start | bytes 294920 | tf_op jit(solution)/shard_map/ppermute | solution.py:296
  120.9 3.6 %collective-permute-done.1 = bf16[1,384,128]{2,1,0:T(8,128)(2,1)S(1)} collective-permute-done((bf16[1,384,128]{2,1,0:T(8,128)(2,1)}, bf16[1,384,128]{2,1,0:T(8,128)(2,1)S(1)}, u32[]{:S(2)}, u32[]{:S(2)}) %collective-permute-start.1) | collective-permute-done | bytes 98336 | tf_op jit(solution)/shard_map/ppermute | solution.py:296
  124.5 1.6 shard_map.129
  126.1 2.8 %collective-permute-start.2 = (bf16[4,48,128]{2,1,0:T(8,128)(2,1)}, bf16[4,48,128]{2,1,0:T(8,128)(2,1)S(1)}, u32[]{:S(2)}, u32[]{:S(2)}) collective-permute-start(bf16[4,48,128]{2,1,0:T(8,128)(2,1)} %get-tuple-element.23), channel_id=1, source_target_pairs={{0,2},{2,0},{1,3},{3,1},{4,6},{6,4},{5,7},{7,5},{8,10},{10,8},{9,1... | collective-permute-start | bytes 147464 | tf_op jit(solution)/shard_map/ppermute | solution.py:296
  128.9 2.2 %collective-permute-done.2 = bf16[4,48,128]{2,1,0:T(8,128)(2,1)S(1)} collective-permute-done((bf16[4,48,128]{2,1,0:T(8,128)(2,1)}, bf16[4,48,128]{2,1,0:T(8,128)(2,1)S(1)}, u32[]{:S(2)}, u32[]{:S(2)}) %collective-permute-start.2) | collective-permute-done | bytes 49184 | tf_op jit(solution)/shard_map/ppermute | solution.py:296
  131.2 1.5 shard_map.130
  132.7 3.8 %collective-permute-start.3 = (bf16[2,48,128]{2,1,0:T(8,128)(2,1)}, bf16[2,48,128]{2,1,0:T(8,128)(2,1)S(1)}, u32[]{:S(2)}, u32[]{:S(2)}) collective-permute-start(bf16[2,48,128]{2,1,0:T(8,128)(2,1)} %get-tuple-element.25), channel_id=1, source_target_pairs={{0,4},{4,0},{1,5},{5,1},{2,6},{6,2},{3,7},{7,3},{8,12},{12,8},{9,1... | collective-permute-start | bytes 73736 | tf_op jit(solution)/shard_map/ppermute | solution.py:296
  136.5 1.6 shard_map.125.match_ref
  138.1 0.0 all-to-all-done.3.rows_ref.in_ref
  138.1 0.0 copy-start
  138.1 0.9 copy-done
  139.0 0.8 shard_map.126
  139.8 8.2 %all-to-all-start.4 = ((bf16[32,8,128]{2,1,0:T(8,128)(2,1)}), bf16[32,8,128]{2,1,0:T(8,128)(2,1)S(1)}, u32[]{:S(2)}, u32[]{:S(2)}) async-start(bf16[32,8,128]{2,1,0:T(8,128)(2,1)} %shard_map.126), calls=%async_computation.4 | async-start | bytes 131072 | tf_op jit(solution)/shard_map/all_to_all | solution.py:292
  148.0 0.0 collective-permute-done.3
  148.0 1.4 shard_map.131
  149.4 7.2 %collective-permute-start.4 = (bf16[1,48,128]{2,1,0:T(8,128)(2,1)}, bf16[1,48,128]{2,1,0:T(8,128)(2,1)S(1)}, u32[]{:S(2)}, u32[]{:S(2)}) collective-permute-start(bf16[1,48,128]{2,1,0:T(8,128)(2,1)} %get-tuple-element.27), channel_id=1, source_target_pairs={{0,8},{8,0},{1,9},{9,1},{2,10},{10,2},{3,11},{11,3},{4,12},{12,4},... | collective-permute-start | bytes 36872 | tf_op jit(solution)/shard_map/ppermute | solution.py:296
  156.6 1.4 collective-permute-done.4.received_ref
  157.9 1.4 shard_map.132
  159.4 5.2 %shard_map.124 = bf16[4,192,1024]{2,1,0:T(8,128)(2,1)} custom-call(bf16[32,48,128]{2,1,0:T(8,128)(2,1)S(1)} %all-to-all-done.3.rows_ref.in_ref, bf16[4,160,1024]{2,1,0:T(8,128)(2,1)} %saved_ref.1), custom_call_target="tpu_custom_call" | custom-call | flops 1000000000 | bytes 3276800 | tf_op jit(solution)/shard_map/pallas_call | solution.py:36
  164.5 0.0 all-to-all-done.4
  164.6 0.6 slice.4
Async XLA Ops:
  0.6 39.2 %copy-start.2 = (bf16[4,1024,192]{1,2,0:T(8,128)(2,1)S(1)}, bf16[4,1024,192]{1,2,0:T(8,128)(2,1)}, u32[]{:S(2)}) copy-start(bf16[4,1024,192]{1,2,0:T(8,128)(2,1)} %param.12) | copy-start | bytes 4718596
  0.6 39.2 %copy-start.3 = (bf16[128,192]{0,1:T(8,128)(2,1)S(1)}, bf16[128,192]{0,1:T(8,128)(2,1)}, u32[]{:S(2)}) copy-start(bf16[128,192]{0,1:T(8,128)(2,1)} %param.9) | copy-start | bytes 147460
  65.5 32.0 %all-to-all-start.2 = ((bf16[8,24,1024]{2,1,0:T(8,128)(2,1)}), bf16[8,24,1024]{2,1,0:T(8,128)(2,1)S(1)}, u32[]{:S(2)}, u32[]{:S(2)}) async-start(bf16[8,24,1024]{2,1,0:T(8,128)(2,1)} %reduce_sum.12), calls=%async_computation.2 | async-start | bytes 786432 | tf_op jit(solution)/shard_map/all_to_all | solution.py:292
  97.5 1.0 copy-start.1
  99.3 38.8 %all-to-all-start.3 = ((bf16[32,48,128]{2,1,0:T(8,128)(2,1)}), bf16[32,48,128]{2,1,0:T(8,128)(2,1)S(1)}, u32[]{:S(2)}, u32[]{:S(2)}) async-start(bf16[32,48,128]{2,1,0:T(8,128)(2,1)} %get-tuple-element.16), calls=%async_computation.3 | async-start | bytes 786432 | tf_op jit(solution)/shard_map/all_to_all | solution.py:292
  112.4 3.5 %collective-permute-start = (bf16[16,48,128]{2,1,0:T(8,128)(2,1)}, bf16[16,48,128]{2,1,0:T(8,128)(2,1)S(1)}, u32[]{:S(2)}, u32[]{:S(2)}) collective-permute-start(bf16[16,48,128]{2,1,0:T(8,128)(2,1)} %get-tuple-element.19), channel_id=1, source_target_pairs={{0,1},{1,0},{2,3},{3,2},{4,5},{5,4},{6,7},{7,6},{8,9},{9,8},{10,11... | collective-permute-start | bytes 589832 | tf_op jit(solution)/shard_map/ppermute | solution.py:296
  117.6 6.9 %collective-permute-start.1 = (bf16[1,384,128]{2,1,0:T(8,128)(2,1)}, bf16[1,384,128]{2,1,0:T(8,128)(2,1)S(1)}, u32[]{:S(2)}, u32[]{:S(2)}) collective-permute-start(bf16[1,384,128]{2,1,0:T(8,128)(2,1)} %get-tuple-element.21), channel_id=1, source_target_pairs={{0,16},{16,0},{1,17},{17,1},{2,18},{18,2},{3,19},{19,3},{4,20},{20... | collective-permute-start | bytes 294920 | tf_op jit(solution)/shard_map/ppermute | solution.py:296
  126.1 5.0 %collective-permute-start.2 = (bf16[4,48,128]{2,1,0:T(8,128)(2,1)}, bf16[4,48,128]{2,1,0:T(8,128)(2,1)S(1)}, u32[]{:S(2)}, u32[]{:S(2)}) collective-permute-start(bf16[4,48,128]{2,1,0:T(8,128)(2,1)} %get-tuple-element.23), channel_id=1, source_target_pairs={{0,2},{2,0},{1,3},{3,1},{4,6},{6,4},{5,7},{7,5},{8,10},{10,8},{9,1... | collective-permute-start | bytes 147464 | tf_op jit(solution)/shard_map/ppermute | solution.py:296
  132.7 15.3 %collective-permute-start.3 = (bf16[2,48,128]{2,1,0:T(8,128)(2,1)}, bf16[2,48,128]{2,1,0:T(8,128)(2,1)S(1)}, u32[]{:S(2)}, u32[]{:S(2)}) collective-permute-start(bf16[2,48,128]{2,1,0:T(8,128)(2,1)} %get-tuple-element.25), channel_id=1, source_target_pairs={{0,4},{4,0},{1,5},{5,1},{2,6},{6,2},{3,7},{7,3},{8,12},{12,8},{9,1... | collective-permute-start | bytes 73736 | tf_op jit(solution)/shard_map/ppermute | solution.py:296
  138.1 0.9 copy-start
  139.8 24.8 %all-to-all-start.4 = ((bf16[32,8,128]{2,1,0:T(8,128)(2,1)}), bf16[32,8,128]{2,1,0:T(8,128)(2,1)S(1)}, u32[]{:S(2)}, u32[]{:S(2)}) async-start(bf16[32,8,128]{2,1,0:T(8,128)(2,1)} %shard_map.126), calls=%async_computation.4 | async-start | bytes 131072 | tf_op jit(solution)/shard_map/all_to_all | solution.py:292
  149.4 8.5 %collective-permute-start.4 = (bf16[1,48,128]{2,1,0:T(8,128)(2,1)}, bf16[1,48,128]{2,1,0:T(8,128)(2,1)S(1)}, u32[]{:S(2)}, u32[]{:S(2)}) collective-permute-start(bf16[1,48,128]{2,1,0:T(8,128)(2,1)} %get-tuple-element.27), channel_id=1, source_target_pairs={{0,8},{8,0},{1,9},{9,1},{2,10},{10,2},{3,11},{11,3},{4,12},{12,4},... | collective-permute-start | bytes 36872 | tf_op jit(solution)/shard_map/ppermute | solution.py:296
